TPU v7x, 32 devices: a whole 2x2x4 slice. The times are simulated.
32 devices in a mesh: seq: 8 (over y, x, core), head: 4 (over z).
Axes of the slice: x: 2, y: 2, z: 4, core: 2. Of those that a mesh axis runs over, the one named last changes fastest.
Arguments:
- incoming_hidden: bfloat16 [8192, 1024], P(('seq', 'head')), may hold values from -6 to 6
- earliest_block_vals: bfloat16 [8192, 1024], P('seq', 'head'), may hold values from -6 to 6
- upstream_sensitivity: bfloat16 [8192, 1024], P(('seq', 'head')), may hold values from -6 to 6
- opening_standardize_factor: float32 [1024], replicated, may hold values from 0.5 to 1.5
- opening_standardize_shift: float32 [1024], replicated, may hold values from -1.5 to 1.5
- attention_lag_blend: float32 [6, 1024], replicated, may hold values from 0 to 1
- acceptor_linear_map: bfloat16 [1024, 1024], P('seq', 'head'), may hold values from -0.1875 to 0.1875
- address_linear_map: bfloat16 [1024, 1024], P('seq', 'head'), may hold values from -0.1875 to 0.1875
- content_linear_map: bfloat16 [1024, 1024], P('seq', 'head'), may hold values from -0.1875 to 0.1875
- fading_narrowing: bfloat16 [1024, 64], P('seq'), may hold values from -0.1875 to 0.1875
- fading_widening: bfloat16 [64, 1024], P('seq', 'head'), may hold values from -0.75 to 0.75
- fading_baseline: float32 [1024], P('head'), may hold values from -12 to -1
- stepsize_narrowing: bfloat16 [1024, 64], P('seq'), may hold values from -0.1875 to 0.1875
- stepsize_widening: bfloat16 [64, 1024], P('seq', 'head'), may hold values from -0.75 to 0.75
- stepsize_baseline: float32 [1024], P('head'), may hold values from -10 to 1
- residual_blend_narrowing: bfloat16 [1024, 32], P('seq'), may hold values from -0.1875 to 0.1875
- residual_blend_widening: bfloat16 [32, 1024], P('seq', 'head'), may hold values from -1 to 1
- residual_blend_baseline: float32 [1024], P('head'), may hold values from -4 to 4
- valve_narrowing: bfloat16 [1024, 128], P('seq'), may hold values from -0.1875 to 0.1875
- valve_widening: bfloat16 [128, 1024], P('seq', 'head'), may hold values from -0.5 to 0.5
- erasing_address_factor: float32 [1024], P('head'), may hold values from 0.3 to 3
- address_rate_portion: float32 [1024], P('head'), may hold values from 0 to 1
- present_extra_factor: float32 [1024], P('head'), may hold values from -1 to 1
- attend_standardize_factor: float32 [1024], P('head'), may hold values from 0.25 to 1.75
- attend_standardize_shift: float32 [1024], P('head'), may hold values from -1.5 to 1.5
- emitted_linear_map: bfloat16 [1024, 1024], P('head', 'seq'), may hold values from -0.1875 to 0.1875
- closing_standardize_factor: float32 [1024], replicated, may hold values from 0.5 to 1.5
- closing_standardize_shift: float32 [1024], replicated, may hold values from -1.5 to 1.5
- feedforward_lag_blend: float32 [1024], replicated, may hold values from 0 to 1
- feedforward_entrance: bfloat16 [1024, 4096], P('seq', 'head'), may hold values from -0.1875 to 0.1875
- feedforward_exit: bfloat16 [4096, 1024], P('head', 'seq'), may hold values from -0.09375 to 0.09375
Outputs:
- hidden_out: bfloat16 [8192, 1024], P(('seq', 'head'))
- incoming_hidden_adjoint: float32 [8192, 1024], P(('seq', 'head'))
- earliest_block_vals_adjoint: float32 [8192, 1024], P('seq', 'head')
- opening_standardize_factor_adj: float32 [1024], replicated
- opening_standardize_shift_adj: float32 [1024], replicated
- attention_lag_blend_adjoint: float32 [5, 1024], replicated
- decay_lag_blend_adjoint: float32 [1024], replicated
- acceptor_linear_map_adjoint: float32 [1024, 1024], P('seq', 'head')
- address_linear_map_adjoint: float32 [1024, 1024], P('seq', 'head')
- content_linear_map_adjoint: float32 [1024, 1024], P('seq', 'head')
- fading_narrowing_adjoint: float32 [1024, 64], P('seq')
- fading_widening_adjoint: float32 [64, 1024], P('seq', 'head')
- fading_baseline_adjoint: float32 [1024], P('head')
- stepsize_narrowing_adjoint: float32 [1024, 64], P('seq')
- stepsize_widening_adjoint: float32 [64, 1024], P('seq', 'head')
- stepsize_baseline_adjoint: float32 [1024], P('head')
- residual_blend_narrowing_adj: float32 [1024, 32], P('seq')
- residual_blend_widening_adj: float32 [32, 1024], P('seq', 'head')
- residual_blend_baseline_adj: float32 [1024], P('head')
- valve_narrowing_adjoint: float32 [1024, 128], P('seq')
- valve_widening_adjoint: float32 [128, 1024], P('seq', 'head')
- erasing_address_factor_adj: float32 [1024], P('head')
- address_rate_portion_adjoint: float32 [1024], P('head')
- present_extra_adjoint: float32 [1024], P('head')
- attend_standardize_factor_adj: float32 [1024], P('head')
- attend_standardize_shift_adj: float32 [1024], P('head')
- emitted_linear_map_adjoint: float32 [1024, 1024], P('head', 'seq')
- closing_standardize_factor_adj: float32 [1024], replicated
- closing_standardize_shift_adj: float32 [1024], replicated
- feedforward_lag_blend_adjoint: float32 [1024], replicated
- feedforward_entrance_adjoint: float32 [1024, 4096], P('seq', 'head')
- feedforward_exit_adjoint: float32 [4096, 1024], P('head', 'seq')
All inputs are finite; a program needn't handle non-finite values.
Results may differ from a plain program's by a relative error of at most 0.028.
Values may be sent and summed in bfloat16 or wider, within the bound.
No kernel may reach another device: no remote copies, remote signals or barrier semaphores. Data moves between devices by JAX's collectives and lax.ppermute only.
A program may use at most 256 MiB of HBM per device.

v0:
```python
import jax
import jax.numpy as jnp
from jax import lax
from jax.sharding import PartitionSpec as P

ATTEND_FEATURES = 64
BLOCK = 64


HIGHEST = lax.Precision.HIGHEST


def shifted(block, axis, distance):
    devices = range(lax.axis_size(axis))
    route = [(i - distance, i) for i in devices if i - distance in devices]
    return lax.ppermute(block, axis, route)


def product(left, right):
    return jnp.dot(left, right, preferred_element_type=jnp.float32)


def cross_rows(left, right):
    return lax.dot_general(
        left, right, (((0,), (0,)), ((), ())), preferred_element_type=jnp.float32
    )


def cross_cols(left, right):
    return lax.dot_general(
        left, right, (((1,), (1,)), ((), ())), preferred_element_type=jnp.float32
    )


def layer_norm(content_tokens, norm_gain, norm_bias):
    row_mean = jnp.mean(content_tokens, axis=-1, keepdims=True)
    centred = content_tokens - row_mean
    row_var = jnp.mean(centred * centred, axis=-1, keepdims=True)
    return centred * lax.rsqrt(row_var + 1e-05) * norm_gain + norm_bias


def prepare(
    acceptor_tokens,
    key_base,
    value_base,
    decay_prod,
    rate_prod,
    blend_prod,
    earliest_block_vals,
    fading_baseline,
    stepsize_baseline,
    residual_blend_baseline,
    erasing_address_factor,
    address_rate_portion,
):
    token_total = acceptor_tokens.shape[0]
    log_decay = -jnp.exp(-jax.nn.softplus(-(fading_baseline + decay_prod)) - 0.5)
    rate_vals = jax.nn.sigmoid(stepsize_baseline + rate_prod)
    blend_vals = jax.nn.sigmoid(residual_blend_baseline + blend_prod)
    content_tokens = value_base + (earliest_block_vals - value_base) * blend_vals
    removal = (key_base * erasing_address_factor).reshape(token_total, -1, ATTEND_FEATURES)
    removal = removal * lax.rsqrt(jnp.sum(removal * removal, axis=-1, keepdims=True) + 1e-06)
    address_signals = key_base * (1.0 + (rate_vals - 1.0) * address_rate_portion)
    return (
        acceptor_tokens.reshape(token_total, -1, ATTEND_FEATURES),
        log_decay.reshape(token_total, -1, ATTEND_FEATURES),
        removal,
        rate_vals.reshape(token_total, -1, ATTEND_FEATURES),
        address_signals.reshape(token_total, -1, ATTEND_FEATURES),
        content_tokens.reshape(token_total, -1, ATTEND_FEATURES),
    )


def wrap_around_rule(
    emitted_tokens,
    acceptor_tokens,
    address_signals,
    content_tokens,
    sigmoid_valve_levels,
    present_extra_factor,
    attend_standardize_factor,
    attend_standardize_shift,
):
    token_total = emitted_tokens.shape[0]
    head_mean = jnp.mean(emitted_tokens, axis=-1, keepdims=True)
    centred = emitted_tokens - head_mean
    head_var = jnp.mean(centred * centred, axis=-1, keepdims=True)
    per_attend_split = (centred * lax.rsqrt(head_var + 0.00064)).reshape(
        token_total, -1
    ) * attend_standardize_factor + attend_standardize_shift
    present_token_extra = (
        jnp.sum(
            acceptor_tokens * address_signals * present_extra_factor.reshape(-1, ATTEND_FEATURES),
            axis=-1,
            keepdims=True,
        )
        * content_tokens
    )
    return (per_attend_split + present_token_extra.reshape(token_total, -1)) * sigmoid_valve_levels


def recurrence_blocks(
    acceptor_tokens, log_decay, removal, rate_vals, address_signals, content_tokens
):
    token_total, head_count, head_width = acceptor_tokens.shape
    block_count = token_total // BLOCK

    def arrange(component_element):
        return component_element.reshape(
            block_count, BLOCK, head_count, component_element.shape[-1]
        ).transpose(0, 2, 1, 3)

    padded_values = jnp.concatenate([jnp.zeros_like(content_tokens), content_tokens], axis=-1)
    inputs = (
        arrange(acceptor_tokens),
        arrange(log_decay),
        arrange(removal),
        arrange(rate_vals),
        arrange(address_signals),
        arrange(padded_values),
    )
    identity = jnp.broadcast_to(
        jnp.eye(head_width, dtype=jnp.float32), (head_count, head_width, head_width)
    )
    start = jnp.concatenate([identity, jnp.zeros_like(identity)], axis=1)
    strict = jnp.tril(jnp.ones((BLOCK, BLOCK), jnp.float32), -1)
    within = jnp.tril(jnp.ones((BLOCK, BLOCK), jnp.float32))
    unit_matrix = jnp.eye(BLOCK, dtype=jnp.float32)

    def one_block(carried_state, block):
        block_recept, block_decay, block_remove, block_rate, block_key, block_value = block
        decay_sum = jnp.cumsum(block_decay, axis=1)
        decay_before = decay_sum - block_decay
        block_end = decay_sum[:, -1:, :]
        pull_left = -block_remove * jnp.exp(decay_before)
        write_base = block_remove * block_rate
        write_right = write_base * jnp.exp(-decay_sum)
        key_right = block_key * jnp.exp(-decay_sum)
        read_left = block_recept * jnp.exp(decay_sum)
        pull_write = jnp.einsum("hck,hdk->hcd", pull_left, write_right, precision=HIGHEST) * strict
        pull_key = jnp.einsum("hck,hdk->hcd", pull_left, key_right, precision=HIGHEST) * strict
        pull_rhs = jnp.einsum(
            "hck,hrk->hcr", pull_left, carried_state, precision=HIGHEST
        ) + jnp.einsum("hcd,hdr->hcr", pull_key, block_value, precision=HIGHEST)
        pulled = lax.linalg.triangular_solve(
            unit_matrix - pull_write, pull_rhs, left_side=True, lower=True, unit_diagonal=True
        )
        read_write = jnp.einsum("hck,hdk->hcd", read_left, write_right, precision=HIGHEST) * within
        read_key = jnp.einsum("hck,hdk->hcd", read_left, key_right, precision=HIGHEST) * within
        output = (
            jnp.einsum("hck,hrk->hcr", read_left, carried_state, precision=HIGHEST)
            + jnp.einsum("hcd,hdr->hcr", read_write, pulled, precision=HIGHEST)
            + jnp.einsum("hcd,hdr->hcr", read_key, block_value, precision=HIGHEST)
        )
        fade_out = jnp.exp(block_end - decay_sum)
        carried_state = (
            carried_state * jnp.exp(block_end)
            + jnp.einsum("hcr,hck->hrk", pulled, write_base * fade_out, precision=HIGHEST)
            + jnp.einsum("hcr,hck->hrk", block_value, block_key * fade_out, precision=HIGHEST)
        )
        return (carried_state, output)

    last_state, emitted_tokens = lax.scan(one_block, start, inputs)
    emitted_tokens = emitted_tokens.transpose(0, 2, 1, 3).reshape(
        token_total, head_count, 2 * head_width
    )
    return (
        emitted_tokens[..., :head_width],
        emitted_tokens[..., head_width:],
        last_state[:, :head_width, :],
        last_state[:, head_width:, :],
    )


def advance(state, transfer_map):
    return jnp.einsum("hij,hjk->hik", state, transfer_map, precision=HIGHEST)


def state_prefix(transfer_map, local_state):

    def relay_step(step_index, carried):
        return shifted(
            (advance(carried, transfer_map) + local_state).astype(jnp.bfloat16), "seq", 1
        ).astype(jnp.float32)

    return lax.fori_loop(0, lax.axis_size("seq") - 1, relay_step, jnp.zeros_like(local_state))


def state_suffix(transfer_map, grad_local):
    flipped = jnp.swapaxes(transfer_map, 1, 2)

    def relay_step(step_index, carried):
        return shifted(
            (advance(carried, flipped) + grad_local).astype(jnp.bfloat16), "seq", -1
        ).astype(jnp.float32)

    return lax.fori_loop(0, lax.axis_size("seq") - 1, relay_step, jnp.zeros_like(grad_local))


def spread_rows(block_rows):
    return lax.all_gather(block_rows, "head", axis=0, tiled=True)


def collect_rows(partial_value):
    return lax.psum_scatter(
        partial_value.astype(jnp.bfloat16), "head", scatter_dimension=0, tiled=True
    ).astype(jnp.float32)


def with_before(token_rows):
    arriving = shifted(token_rows[-1:], "seq", 1)
    return jnp.concatenate([arriving, token_rows[:-1]], axis=0)


def fold_before(grad_rows, grad_before):
    arriving = shifted(grad_before[:1], "seq", -1)
    return grad_rows + jnp.concatenate([grad_before[1:], arriving], axis=0)


def gather_weights(
    acceptor_linear_map,
    address_linear_map,
    content_linear_map,
    emitted_linear_map,
    fading_narrowing,
    stepsize_narrowing,
    residual_blend_narrowing,
    valve_narrowing,
    fading_widening,
    stepsize_widening,
    residual_blend_widening,
    valve_widening,
    feedforward_entrance,
    feedforward_exit,
):
    return (
        lax.all_gather(acceptor_linear_map, "seq", axis=0, tiled=True),
        lax.all_gather(address_linear_map, "seq", axis=0, tiled=True),
        lax.all_gather(content_linear_map, "seq", axis=0, tiled=True),
        lax.all_gather(emitted_linear_map, "seq", axis=1, tiled=True),
        lax.all_gather(fading_narrowing, "seq", axis=0, tiled=True),
        lax.all_gather(stepsize_narrowing, "seq", axis=0, tiled=True),
        lax.all_gather(residual_blend_narrowing, "seq", axis=0, tiled=True),
        lax.all_gather(valve_narrowing, "seq", axis=0, tiled=True),
        lax.all_gather(fading_widening, "seq", axis=0, tiled=True),
        lax.all_gather(stepsize_widening, "seq", axis=0, tiled=True),
        lax.all_gather(residual_blend_widening, "seq", axis=0, tiled=True),
        lax.all_gather(valve_widening, "seq", axis=0, tiled=True),
        lax.all_gather(feedforward_entrance, "seq", axis=0, tiled=True),
        lax.all_gather(feedforward_exit, "seq", axis=1, tiled=True),
    )


def body(
    incoming_hidden,
    earliest_block_vals,
    upstream_sensitivity,
    opening_standardize_factor,
    opening_standardize_shift,
    attention_lag_blend,
    acceptor_linear_map,
    address_linear_map,
    content_linear_map,
    fading_narrowing,
    fading_widening,
    fading_baseline,
    stepsize_narrowing,
    stepsize_widening,
    stepsize_baseline,
    residual_blend_narrowing,
    residual_blend_widening,
    residual_blend_baseline,
    valve_narrowing,
    valve_widening,
    erasing_address_factor,
    address_rate_portion,
    present_extra_factor,
    attend_standardize_factor,
    attend_standardize_shift,
    emitted_linear_map,
    closing_standardize_factor,
    closing_standardize_shift,
    feedforward_lag_blend,
    feedforward_entrance,
    feedforward_exit,
):
    (
        full_recept,
        full_key,
        full_value,
        full_output,
        full_decay_down,
        full_rate_down,
        full_blend_down,
        full_gate_down,
        full_decay_up,
        full_rate_up,
        full_blend_up,
        full_gate_up,
        full_channel_key,
        full_channel_value,
    ) = gather_weights(
        acceptor_linear_map,
        address_linear_map,
        content_linear_map,
        emitted_linear_map,
        fading_narrowing,
        stepsize_narrowing,
        residual_blend_narrowing,
        valve_narrowing,
        fading_widening,
        stepsize_widening,
        residual_blend_widening,
        valve_widening,
        feedforward_entrance,
        feedforward_exit,
    )
    own_rows = incoming_hidden.shape[0]
    row_start = lax.axis_index("head") * own_rows
    residual_in = incoming_hidden.astype(jnp.float32)
    normed_front, front_back = jax.vjp(
        layer_norm, residual_in, opening_standardize_factor, opening_standardize_shift
    )
    normed = spread_rows(normed_front.astype(jnp.bfloat16))
    normed_wide = normed.astype(jnp.float32)
    shift_delta = with_before(normed).astype(jnp.float32) - normed_wide
    mixed_in = (normed_wide[None] + shift_delta[None] * attention_lag_blend[:, None, :]).astype(
        jnp.bfloat16
    )
    acceptor_tokens = product(mixed_in[0], full_recept)
    key_base = product(mixed_in[2], full_key)
    value_base = product(mixed_in[3], full_value)
    decay_lat = product(mixed_in[1], full_decay_down)
    decay_tanh = jnp.tanh(decay_lat).astype(jnp.bfloat16)
    rate_lat = product(mixed_in[4], full_rate_down).astype(jnp.bfloat16)
    blend_lat = product(mixed_in[3], full_blend_down).astype(jnp.bfloat16)
    gate_pre = product(mixed_in[5], full_gate_down)
    gate_lat = jax.nn.sigmoid(gate_pre).astype(jnp.bfloat16)
    decay_prod = product(decay_tanh, full_decay_up)
    rate_prod = product(rate_lat, full_rate_up)
    blend_prod = product(blend_lat, full_blend_up)
    sigmoid_valve_levels = product(gate_lat, full_gate_up)
    scan_operands, prepare_back = jax.vjp(
        prepare,
        acceptor_tokens,
        key_base,
        value_base,
        decay_prod,
        rate_prod,
        blend_prod,
        earliest_block_vals.astype(jnp.float32),
        fading_baseline,
        stepsize_baseline,
        residual_blend_baseline,
        erasing_address_factor,
        address_rate_portion,
    )
    core_vals, core_back = jax.vjp(recurrence_blocks, *scan_operands)
    query_map, local_out, transfer_map, local_state = core_vals
    incoming = state_prefix(transfer_map, local_state)
    emitted_tokens = jnp.einsum("thj,hij->thi", query_map, incoming, precision=HIGHEST) + local_out
    branch_wide, finish_back = jax.vjp(
        wrap_around_rule,
        emitted_tokens,
        scan_operands[0],
        scan_operands[4],
        scan_operands[5],
        sigmoid_valve_levels,
        present_extra_factor,
        attend_standardize_factor,
        attend_standardize_shift,
    )
    auxiliary_path = branch_wide.astype(jnp.bfloat16)
    middle = residual_in + collect_rows(product(auxiliary_path, full_output))
    normed_mid_front, middle_back = jax.vjp(
        layer_norm, middle, closing_standardize_factor, closing_standardize_shift
    )
    normed_mid = spread_rows(normed_mid_front.astype(jnp.bfloat16))
    mid_wide = normed_mid.astype(jnp.float32)
    mid_delta = with_before(normed_mid).astype(jnp.float32) - mid_wide
    keyed_in = (mid_wide + mid_delta * feedforward_lag_blend).astype(jnp.bfloat16)
    hidden_pre = product(keyed_in, full_channel_key)
    hidden = jnp.square(jax.nn.relu(hidden_pre)).astype(jnp.bfloat16)
    result = middle + collect_rows(product(hidden, full_channel_value))
    grad_top = spread_rows(upstream_sensitivity)
    feedforward_exit_adjoint = cross_rows(hidden, grad_top)
    grad_pre = (cross_cols(grad_top, full_channel_value) * 2.0 * jax.nn.relu(hidden_pre)).astype(
        jnp.bfloat16
    )
    feedforward_entrance_adjoint = cross_rows(keyed_in, grad_pre)
    grad_keyed = cross_cols(grad_pre, full_channel_key)
    feedforward_lag_blend_adjoint = jnp.sum(grad_keyed * mid_delta, axis=0)
    grad_mid_rows = fold_before(
        grad_keyed * (1.0 - feedforward_lag_blend), grad_keyed * feedforward_lag_blend
    )
    grad_middle_in, closing_standardize_factor_adj, closing_standardize_shift_adj = middle_back(
        collect_rows(grad_mid_rows)
    )
    grad_middle = upstream_sensitivity.astype(jnp.float32) + grad_middle_in
    grad_attend = spread_rows(grad_middle.astype(jnp.bfloat16))
    emitted_linear_map_adjoint = cross_rows(auxiliary_path, grad_attend)
    grad_branch = cross_cols(grad_attend, full_output)
    (
        grad_outputs,
        grad_recept_extra,
        grad_keys_extra,
        grad_values_extra,
        grad_gate_vals,
        present_extra_adjoint,
        attend_standardize_factor_adj,
        attend_standardize_shift_adj,
    ) = finish_back(grad_branch)
    grad_local = jnp.einsum("thi,thj->hij", grad_outputs, query_map, precision=HIGHEST)
    grad_later = state_suffix(transfer_map, grad_local)
    grad_query = jnp.einsum("thi,hij->thj", grad_outputs, incoming, precision=HIGHEST)
    grad_transfer = jnp.einsum("hki,hkj->hij", incoming, grad_later, precision=HIGHEST)
    grad_kernel = core_back((grad_query, grad_outputs, grad_transfer, grad_later))
    grad_kernel = (
        grad_kernel[0] + grad_recept_extra,
        grad_kernel[1],
        grad_kernel[2],
        grad_kernel[3],
        grad_kernel[4] + grad_keys_extra,
        grad_kernel[5] + grad_values_extra,
    )
    (
        grad_recept,
        grad_key_base,
        grad_value_base,
        grad_decay_prod,
        grad_rate_prod,
        grad_blend_prod,
        earliest_block_vals_adjoint,
        fading_baseline_adjoint,
        stepsize_baseline_adjoint,
        residual_blend_baseline_adj,
        erasing_address_factor_adj,
        address_rate_portion_adjoint,
    ) = prepare_back(grad_kernel)
    recept_back = grad_recept.astype(jnp.bfloat16)
    key_back = grad_key_base.astype(jnp.bfloat16)
    value_back = grad_value_base.astype(jnp.bfloat16)
    decay_prod_back = grad_decay_prod.astype(jnp.bfloat16)
    rate_prod_back = grad_rate_prod.astype(jnp.bfloat16)
    blend_prod_back = grad_blend_prod.astype(jnp.bfloat16)
    gate_back = grad_gate_vals.astype(jnp.bfloat16)
    acceptor_linear_map_adjoint = cross_rows(mixed_in[0], recept_back)
    address_linear_map_adjoint = cross_rows(mixed_in[2], key_back)
    content_linear_map_adjoint = cross_rows(mixed_in[3], value_back)
    fading_widening_adjoint = cross_rows(decay_tanh, decay_prod_back)
    stepsize_widening_adjoint = cross_rows(rate_lat, rate_prod_back)
    residual_blend_widening_adj = cross_rows(blend_lat, blend_prod_back)
    valve_widening_adjoint = cross_rows(gate_lat, gate_back)
    decay_tanh_grad, rate_lat_grad, blend_lat_grad, gate_lat_grad = (
        lax.psum(cross_cols(decay_prod_back, full_decay_up).astype(jnp.bfloat16), "head").astype(
            jnp.float32
        ),
        lax.psum(cross_cols(rate_prod_back, full_rate_up).astype(jnp.bfloat16), "head").astype(
            jnp.float32
        ),
        lax.psum(cross_cols(blend_prod_back, full_blend_up).astype(jnp.bfloat16), "head").astype(
            jnp.float32
        ),
        lax.psum(cross_cols(gate_back, full_gate_up).astype(jnp.bfloat16), "head").astype(
            jnp.float32
        ),
    )
    tanh_wide = jnp.tanh(decay_lat)
    decay_lat_back = (decay_tanh_grad * (1.0 - tanh_wide * tanh_wide)).astype(jnp.bfloat16)
    rate_lat_back = rate_lat_grad.astype(jnp.bfloat16)
    blend_lat_back = blend_lat_grad.astype(jnp.bfloat16)
    gate_sigmoid = jax.nn.sigmoid(gate_pre)
    gate_pre_back = (gate_lat_grad * gate_sigmoid * (1.0 - gate_sigmoid)).astype(jnp.bfloat16)
    fading_narrowing_adjoint = cross_rows(mixed_in[1], decay_lat_back)
    stepsize_narrowing_adjoint = cross_rows(mixed_in[4], rate_lat_back)
    residual_blend_narrowing_adj = cross_rows(mixed_in[3], blend_lat_back)
    valve_narrowing_adjoint = cross_rows(mixed_in[5], gate_pre_back)
    zero_rows = jnp.zeros(normed_wide.shape, jnp.float32)

    def own_part(lat_back, full_down):
        piece = cross_cols(lax.dynamic_slice_in_dim(lat_back, row_start, own_rows, 0), full_down)
        return lax.dynamic_update_slice_in_dim(zero_rows, piece, row_start, 0)

    grad_mixed = jnp.stack(
        [
            cross_cols(recept_back, full_recept),
            own_part(decay_lat_back, full_decay_down),
            cross_cols(key_back, full_key),
            cross_cols(value_back, full_value) + own_part(blend_lat_back, full_blend_down),
            own_part(rate_lat_back, full_rate_down),
            own_part(gate_pre_back, full_gate_down),
        ]
    )
    shift_sums = jnp.sum(grad_mixed * shift_delta[None], axis=1)
    grad_normed = fold_before(
        jnp.sum(grad_mixed * (1.0 - attention_lag_blend[:, None, :]), axis=0),
        jnp.sum(grad_mixed * attention_lag_blend[:, None, :], axis=0),
    )
    grad_front_in, opening_standardize_factor_adj, opening_standardize_shift_adj = front_back(
        collect_rows(grad_normed)
    )
    incoming_hidden_adjoint = grad_middle + grad_front_in
    (
        opening_standardize_factor_adj,
        opening_standardize_shift_adj,
        shift_sums,
        closing_standardize_factor_adj,
        closing_standardize_shift_adj,
        feedforward_lag_blend_adjoint,
    ) = lax.psum(
        (
            opening_standardize_factor_adj,
            opening_standardize_shift_adj,
            shift_sums,
            closing_standardize_factor_adj,
            closing_standardize_shift_adj,
            feedforward_lag_blend_adjoint,
        ),
        ("seq", "head"),
    )
    attention_lag_blend_adjoint = jnp.concatenate([shift_sums[:1], shift_sums[2:]], axis=0)
    decay_lag_blend_adjoint = shift_sums[1]
    (
        fading_baseline_adjoint,
        stepsize_baseline_adjoint,
        residual_blend_baseline_adj,
        erasing_address_factor_adj,
        address_rate_portion_adjoint,
        present_extra_adjoint,
        attend_standardize_factor_adj,
        attend_standardize_shift_adj,
    ) = lax.psum(
        (
            fading_baseline_adjoint,
            stepsize_baseline_adjoint,
            residual_blend_baseline_adj,
            erasing_address_factor_adj,
            address_rate_portion_adjoint,
            present_extra_adjoint,
            attend_standardize_factor_adj,
            attend_standardize_shift_adj,
        ),
        "seq",
    )
    (
        acceptor_linear_map_adjoint,
        address_linear_map_adjoint,
        content_linear_map_adjoint,
        emitted_linear_map_adjoint,
        fading_narrowing_adjoint,
        stepsize_narrowing_adjoint,
        residual_blend_narrowing_adj,
        valve_narrowing_adjoint,
        fading_widening_adjoint,
        stepsize_widening_adjoint,
        residual_blend_widening_adj,
        valve_widening_adjoint,
        feedforward_entrance_adjoint,
        feedforward_exit_adjoint,
    ) = (
        lax.psum_scatter(
            acceptor_linear_map_adjoint.astype(jnp.bfloat16), "seq", scatter_dimension=0, tiled=True
        ).astype(jnp.float32),
        lax.psum_scatter(
            address_linear_map_adjoint.astype(jnp.bfloat16), "seq", scatter_dimension=0, tiled=True
        ).astype(jnp.float32),
        lax.psum_scatter(
            content_linear_map_adjoint.astype(jnp.bfloat16), "seq", scatter_dimension=0, tiled=True
        ).astype(jnp.float32),
        lax.psum_scatter(
            emitted_linear_map_adjoint.astype(jnp.bfloat16), "seq", scatter_dimension=1, tiled=True
        ).astype(jnp.float32),
        lax.psum_scatter(
            fading_narrowing_adjoint.astype(jnp.bfloat16), "seq", scatter_dimension=0, tiled=True
        ).astype(jnp.float32),
        lax.psum_scatter(
            stepsize_narrowing_adjoint.astype(jnp.bfloat16), "seq", scatter_dimension=0, tiled=True
        ).astype(jnp.float32),
        lax.psum_scatter(
            residual_blend_narrowing_adj.astype(jnp.bfloat16),
            "seq",
            scatter_dimension=0,
            tiled=True,
        ).astype(jnp.float32),
        lax.psum_scatter(
            valve_narrowing_adjoint.astype(jnp.bfloat16), "seq", scatter_dimension=0, tiled=True
        ).astype(jnp.float32),
        lax.psum_scatter(
            fading_widening_adjoint.astype(jnp.bfloat16), "seq", scatter_dimension=0, tiled=True
        ).astype(jnp.float32),
        lax.psum_scatter(
            stepsize_widening_adjoint.astype(jnp.bfloat16), "seq", scatter_dimension=0, tiled=True
        ).astype(jnp.float32),
        lax.psum_scatter(
            residual_blend_widening_adj.astype(jnp.bfloat16), "seq", scatter_dimension=0, tiled=True
        ).astype(jnp.float32),
        lax.psum_scatter(
            valve_widening_adjoint.astype(jnp.bfloat16), "seq", scatter_dimension=0, tiled=True
        ).astype(jnp.float32),
        lax.psum_scatter(
            feedforward_entrance_adjoint.astype(jnp.bfloat16),
            "seq",
            scatter_dimension=0,
            tiled=True,
        ).astype(jnp.float32),
        lax.psum_scatter(
            feedforward_exit_adjoint.astype(jnp.bfloat16), "seq", scatter_dimension=1, tiled=True
        ).astype(jnp.float32),
    )
    return (
        result.astype(jnp.bfloat16),
        incoming_hidden_adjoint,
        earliest_block_vals_adjoint,
        opening_standardize_factor_adj,
        opening_standardize_shift_adj,
        attention_lag_blend_adjoint,
        decay_lag_blend_adjoint,
        acceptor_linear_map_adjoint,
        address_linear_map_adjoint,
        content_linear_map_adjoint,
        fading_narrowing_adjoint,
        fading_widening_adjoint,
        fading_baseline_adjoint,
        stepsize_narrowing_adjoint,
        stepsize_widening_adjoint,
        stepsize_baseline_adjoint,
        residual_blend_narrowing_adj,
        residual_blend_widening_adj,
        residual_blend_baseline_adj,
        valve_narrowing_adjoint,
        valve_widening_adjoint,
        erasing_address_factor_adj,
        address_rate_portion_adjoint,
        present_extra_adjoint,
        attend_standardize_factor_adj,
        attend_standardize_shift_adj,
        emitted_linear_map_adjoint,
        closing_standardize_factor_adj,
        closing_standardize_shift_adj,
        feedforward_lag_blend_adjoint,
        feedforward_entrance_adjoint,
        feedforward_exit_adjoint,
    )


def solution(mesh):
    in_specs = (
        P(("seq", "head"), None),
        P("seq", "head"),
        P(("seq", "head"), None),
        P(),
        P(),
        P(),
        P("seq", "head"),
        P("seq", "head"),
        P("seq", "head"),
        P("seq", None),
        P("seq", "head"),
        P("head"),
        P("seq", None),
        P("seq", "head"),
        P("head"),
        P("seq", None),
        P("seq", "head"),
        P("head"),
        P("seq", None),
        P("seq", "head"),
        P("head"),
        P("head"),
        P("head"),
        P("head"),
        P("head"),
        P("head", "seq"),
        P(),
        P(),
        P(),
        P("seq", "head"),
        P("head", "seq"),
    )
    out_specs = (
        P(("seq", "head"), None),
        P(("seq", "head"), None),
        P("seq", "head"),
        P(),
        P(),
        P(),
        P(),
        P("seq", "head"),
        P("seq", "head"),
        P("seq", "head"),
        P("seq", None),
        P("seq", "head"),
        P("head"),
        P("seq", None),
        P("seq", "head"),
        P("head"),
        P("seq", None),
        P("seq", "head"),
        P("head"),
        P("seq", None),
        P("seq", "head"),
        P("head"),
        P("head"),
        P("head"),
        P("head"),
        P("head"),
        P("head", "seq"),
        P(),
        P(),
        P(),
        P("seq", "head"),
        P("head", "seq"),
    )
    return jax.shard_map(body, mesh=mesh, in_specs=in_specs, out_specs=out_specs, check_vma=False)
```

profile of v0, /device:TPU:0, one launch (start us, length us, event | category | flops | bytes accessed | tf_op | source)
XLA Modules:
  0.0 3031.4 jit_solution(6985415200635997676)
XLA Ops:
  220.2 660.5 %while.107 = (s32[]{:T(128)}, f32[4,128,64]{1,2,0:T(8,128)S(1)}, f32[16,4,64,128]{3,2,0,1:T(8,128)S(1)}, f32[16,4,64,64]{3,2,1,0:T(8,128)}, f32[16,4,64,64]{3,2,...) while((s32[]{:T(128)}, f32[4,128,64]{1,2,0:T(8,128)S(1)}, ...), condition=%wide.region_5.6_spmd.clone.clone, body=%wide.region_3.5_spmd.clone.clone.sunk | while | flops 253530176 | bytes 9728537 | solution.py:163
  226.4 20.4 custom-call.31
  267.7 20.4 custom-call.31
  309.0 20.4 custom-call.31
  350.3 20.4 custom-call.31
  391.6 20.4 custom-call.31
  432.9 20.4 custom-call.31
  886.0 37.5 %while.109 = (s32[]{:T(128)}, f32[4,64,64]{2,1,0:T(8,128)S(1)}, f32[4,64,64]{2,1,0:T(8,128)S(1)}, f32[4,64,64]{2,1,0:T(8,128)S(1)}, s32[]{:T(128)}, /*index=5*/s32[]{:T(128)}) while((s32[]{:T(128)}, f32[4,64,64]{2,1,0:T(8,128)S(1)}, f32[4,64,64]{2,1,0:T(8,128)S(1)}, f32[4,64,64]{2,1,0:T(8,128)S(1)}, s32[]{:T(128)}, ...), condition=%wide.region_7.8_spmd.clone, body=%wide.region_6.7_spmd.clone.sunk | while | flops 12648451 | bytes 458871 | solution.py:186
  936.3 53.8 %reduce-scatter.28.cloned.1.call-done = bf16[256,1024]{1,0:T(8,128)(2,1)} async-done(((bf16[1024,1024]{1,0:T(8,128)(2,1)}), bf16[256,1024]{1,0:T(8,128)(2,1)}) %reduce-scatter.28.cloned.1.call-update) | async-done | bytes 524304 | tf_op jit(solution)/shard_map/reduce_scatter | solution.py:205
  995.8 43.2 %all-gather.10.cloned.1.call-done = bf16[1024,1024]{1,0:T(8,128)(2,1)} async-done(((bf16[256,1024]{1,0:T(8,128)(2,1)}), bf16[1024,1024]{1,0:T(8,128)(2,1)}) %all-gather.10.cloned.1.call-update) | async-done | bytes 2097168 | tf_op jit(solution)/shard_map/all_gather | solution.py:201
  1041.3 26.1 all-gather.12.cloned.1.call-done
  1074.7 39.8 %all-gather.16.cloned.1.call-done = bf16[1024,1024]{1,0:T(8,128)(2,1)} async-done(((bf16[256,1024]{1,0:T(8,128)(2,1)}), bf16[1024,1024]{1,0:T(8,128)(2,1)}) %all-gather.16.cloned.1.call-update) | async-done | bytes 2097168 | tf_op jit(solution)/shard_map/all_gather | solution.py:201
  1114.5 28.7 all-gather.14.cloned.1.call-done
  1164.8 39.7 %reduce-scatter.32.cloned.1.call-done = bf16[256,1024]{1,0:T(8,128)(2,1)} async-done(((bf16[1024,1024]{1,0:T(8,128)(2,1)}), bf16[256,1024]{1,0:T(8,128)(2,1)}) %reduce-scatter.32.cloned.1.call-update) | async-done | bytes 524304 | tf_op jit(solution)/shard_map/reduce_scatter | solution.py:205
  1206.7 43.0 %reduce-scatter.30.cloned.1.call-done = bf16[256,1024]{1,0:T(8,128)(2,1)} async-done(((bf16[1024,1024]{1,0:T(8,128)(2,1)}), bf16[256,1024]{1,0:T(8,128)(2,1)}) %reduce-scatter.30.cloned.1.call-update) | async-done | bytes 524304 | tf_op jit(solution)/shard_map/reduce_scatter | solution.py:205
  1255.0 44.3 %all-gather.18.cloned.1.call-done = bf16[1024,1024]{1,0:T(8,128)(2,1)} async-done(((bf16[256,1024]{1,0:T(8,128)(2,1)}), bf16[1024,1024]{1,0:T(8,128)(2,1)}) %all-gather.18.cloned.1.call-update) | async-done | bytes 2097168 | tf_op jit(solution)/shard_map/all_gather | solution.py:201
  1309.8 57.6 %while.110 = (s32[]{:T(128)}, f32[4,64,64]{2,1,0:T(8,128)S(1)}, f32[4,64,64]{2,1,0:T(8,128)S(1)}, f32[4,64,64]{2,1,0:T(8,128)}, s32[]{:T(128)}, /*index=5*/s32[]{:T(128)}) while((s32[]{:T(128)}, f32[4,64,64]{2,1,0:T(8,128)S(1)}, f32[4,64,64]{2,1,0:T(8,128)S(1)}, f32[4,64,64]{2,1,0:T(8,128)}, s32[]{:T(128)}, ...), condition=%wide.region_21.22_spmd.clone, body=%wide.region_20.21_spmd.clone.sunk | while | flops 12648451 | bytes 458871 | solution.py:197
  1384.0 954.1 %while.108 = (s32[]{:T(128)}, f32[4,128,64]{1,2,0:T(8,128)S(1)}, f32[16,4,64,64]{3,2,1,0:T(8,128)}, f32[16,4,64,64]{3,2,1,0:T(8,128)}, f32[16,4,64,64]{3,2,1,0:T...) while((s32[]{:T(128)}, f32[4,128,64]{1,2,0:T(8,128)S(1)}, ...), condition=%wide.region_26.27_spmd.clone.clone, body=%wide.region_22.26_spmd.clone.clone.sunk | while | flops 518074432 | bytes 13143201 | solution.py:163
  2418.5 23.1 all-reduce.13.cloned.1.call-done
  2546.7 22.5 all-reduce.7
  2571.1 28.6 reduce-scatter.42.cloned.1.call-done
  2601.0 35.1 %reduce-scatter.48.cloned.1.call-done = bf16[16,256]{1,0:T(8,128)(2,1)} async-done(((bf16[128,256]{1,0:T(8,128)(2,1)}), bf16[16,256]{1,0:T(8,128)(2,1)}) %reduce-scatter.48.cloned.1.call-update) | async-done | bytes 8208 | tf_op jit(solution)/shard_map/reduce_scatter | solution.py:597
  2637.4 35.3 %reduce-scatter.56.cloned.1.call-done = bf16[128,32]{1,0:T(8,128)(2,1)} async-done(((bf16[1024,32]{1,0:T(8,128)(2,1)}), bf16[128,32]{1,0:T(8,128)(2,1)}) %reduce-scatter.56.cloned.1.call-update) | async-done | bytes 8208
  2674.2 35.1 %reduce-scatter.52.cloned.1.call-done = bf16[128,64]{1,0:T(8,128)(2,1)} async-done(((bf16[1024,64]{1,0:T(8,128)(2,1)}), bf16[128,64]{1,0:T(8,128)(2,1)}) %reduce-scatter.52.cloned.1.call-update) | async-done | bytes 16400
  2710.8 35.1 %reduce-scatter.54.cloned.1.call-done = bf16[128,64]{1,0:T(8,128)(2,1)} async-done(((bf16[1024,64]{1,0:T(8,128)(2,1)}), bf16[128,64]{1,0:T(8,128)(2,1)}) %reduce-scatter.54.cloned.1.call-update) | async-done | bytes 16400
  2747.4 35.7 %reduce-scatter.58.cloned.1.call-done = bf16[128,256]{1,0:T(8,128)(2,1)} async-done(((bf16[1024,256]{1,0:T(8,128)(2,1)}), bf16[128,256]{1,0:T(8,128)(2,1)}) %reduce-scatter.58.cloned.1.call-update) | async-done | bytes 65552
  2784.7 35.4 %reduce-scatter.38.cloned.1.call-done = bf16[128,256]{1,0:T(8,128)(2,1)} async-done(((bf16[1024,256]{1,0:T(8,128)(2,1)}), bf16[128,256]{1,0:T(8,128)(2,1)}) %reduce-scatter.38.cloned.1.call-update) | async-done | bytes 65552 | tf_op jit(solution)/shard_map/reduce_scatter | solution.py:564
  2821.6 35.7 %reduce-scatter.40.cloned.1.call-done = bf16[128,256]{1,0:T(8,128)(2,1)} async-done(((bf16[1024,256]{1,0:T(8,128)(2,1)}), bf16[128,256]{1,0:T(8,128)(2,1)}) %reduce-scatter.40.cloned.1.call-update) | async-done | bytes 65552 | tf_op jit(solution)/shard_map/reduce_scatter | solution.py:567
  2858.9 36.3 %reduce-scatter.36.cloned.1.call-done = bf16[128,256]{1,0:T(8,128)(2,1)} async-done(((bf16[1024,256]{1,0:T(8,128)(2,1)}), bf16[128,256]{1,0:T(8,128)(2,1)}) %reduce-scatter.36.cloned.1.call-update) | async-done | bytes 65552 | tf_op jit(solution)/shard_map/reduce_scatter | solution.py:561
  2896.6 35.3 %reduce-scatter.46.cloned.1.call-done = bf16[128,128]{1,0:T(8,128)(2,1)} async-done(((bf16[1024,128]{1,0:T(8,128)(2,1)}), bf16[128,128]{1,0:T(8,128)(2,1)}) %reduce-scatter.46.cloned.1.call-update) | async-done | bytes 32784 | tf_op jit(solution)/shard_map/reduce_scatter | solution.py:585
  2933.3 44.4 %reduce-scatter.34.cloned.1.call-done = bf16[256,1024]{1,0:T(8,128)(2,1)} async-done(((bf16[1024,1024]{1,0:T(8,128)(2,1)}), bf16[256,1024]{1,0:T(8,128)(2,1)}) %reduce-scatter.34.cloned.1.call-update) | async-done | bytes 524304 | tf_op jit(solution)/shard_map/reduce_scatter | solution.py:205
  2980.9 40.7 %all-reduce.8 = (f32[1024]{0:T(1024)}, f32[1024]{0:T(1024)}, f32[6,1024]{1,0:T(8,128)S(1)}, f32[1024]{0:T(1024)}, f32[1024]{0:T(1024)}, /*index=5*/f32[1024]{0:T(1024)}) all-reduce(f32[1024]{0:T(1024)S(1)} %get-tuple-element.1993, f32[1024]{0:T(1024)S(1)} %get-tuple-element.2000, ...), channel_id=1, replica_groups=mesh['seq'=8,'head'=4] {'seq','head'}, use_global_device_ids=true, to_apply=%region_39.40 | all-reduce | flops 11264 | bytes 90112 | tf_op jit(solution)/shard_map/psum | solution.py:510
  (1676 shorter events, 2089.3 us)
Async XLA Ops:
  7.3 108.8 %all-gather.8.cloned.1.call-start = ((), (), s32[]{:S(2)}) async-start(), calls=%async_computation.17 | async-start | bytes 2621440 | tf_op jit(solution)/shard_map/all_gather | solution.py:201
  12.2 978.0 %reduce-scatter.28.cloned.1.call-start = ((), (), s32[]{:S(2)}) async-start(), calls=%async_computation.18 | async-start | bytes 2621440 | tf_op jit(solution)/shard_map/reduce_scatter | solution.py:205
  116.9 14.4 collective-permute-start.2
  900.0 5.6 collective-permute-start
  936.3 102.7 %all-gather.10.cloned.1.call-start = ((), (), s32[]{:S(2)}) async-start(), calls=%async_computation.19 | async-start | bytes 2621440 | tf_op jit(solution)/shard_map/all_gather | solution.py:201
  994.0 73.4 %all-gather.12.cloned.1.call-start = ((), (), s32[]{:S(2)}) async-start(), calls=%async_computation.20 | async-start | bytes 2359296 | tf_op jit(solution)/shard_map/all_gather | solution.py:249
  994.6 119.9 %all-gather.16.cloned.1.call-start = ((), (), s32[]{:S(2)}) async-start(), calls=%async_computation.23 | async-start | bytes 2621440 | tf_op jit(solution)/shard_map/all_gather | solution.py:201
  995.2 148.0 %all-gather.14.cloned.1.call-start = ((), (), s32[]{:S(2)}) async-start(), calls=%async_computation.21 | async-start | bytes 2359296 | tf_op jit(solution)/shard_map/all_gather | solution.py:250
  995.8 208.8 %reduce-scatter.32.cloned.1.call-start = ((), (), s32[]{:S(2)}) async-start(), calls=%async_computation.24 | async-start | bytes 2621440 | tf_op jit(solution)/shard_map/reduce_scatter | solution.py:205
  1039.8 27.6 collective-permute-start.3
  1158.1 91.6 %reduce-scatter.30.cloned.1.call-start = ((), (), s32[]{:S(2)}) async-start(), calls=%async_computation.22 | async-start | bytes 2621440 | tf_op jit(solution)/shard_map/reduce_scatter | solution.py:205
  1164.8 134.4 %all-gather.18.cloned.1.call-start = ((), (), s32[]{:S(2)}) async-start(), calls=%async_computation.25 | async-start | bytes 2621440 | tf_op jit(solution)/shard_map/all_gather | solution.py:201
  1254.2 1187.4 %all-reduce.13.cloned.1.call-start = ((), (), s32[]{:S(2)}) async-start(), calls=%async_computation.40 | async-start | bytes 1179648 | tf_op jit(solution)/shard_map/psum | solution.py:455
  1326.1 5.9 collective-permute-start.1
  1334.6 5.9 collective-permute-start.1
  1343.2 5.9 collective-permute-start.1
  1351.7 5.9 collective-permute-start.1
  1360.3 6.3 collective-permute-start.1
  2395.5 121.7 %reduce-scatter.60.cloned.1.call-start = ((), (), s32[]{:S(2)}) async-start(), calls=%async_computation.39 | async-start | bytes 2359296
  2406.1 123.8 %reduce-scatter.50.cloned.1.call-start = ((), (), s32[]{:S(2)}) async-start(), calls=%async_computation.34 | async-start | bytes 2359296 | tf_op jit(solution)/shard_map/reduce_scatter | solution.py:600
  2413.6 156.2 %reduce-scatter.44.cloned.1.call-start = ((), (), s32[]{:S(2)}) async-start(), calls=%async_computation.31 | async-start | bytes 36864 | tf_op jit(solution)/shard_map/reduce_scatter | solution.py:591
  2415.5 184.2 %reduce-scatter.42.cloned.1.call-start = ((), (), s32[]{:S(2)}) async-start(), calls=%async_computation.30 | async-start | bytes 36864 | tf_op jit(solution)/shard_map/reduce_scatter | solution.py:588
  2416.4 219.7 %reduce-scatter.48.cloned.1.call-start = ((), (), s32[]{:S(2)}) async-start(), calls=%async_computation.33 | async-start | bytes 73728 | tf_op jit(solution)/shard_map/reduce_scatter | solution.py:597
  2418.5 254.2 %reduce-scatter.56.cloned.1.call-start = ((), (), s32[]{:S(2)}) async-start(), calls=%async_computation.37 | async-start | bytes 294912
  2444.7 264.6 %reduce-scatter.52.cloned.1.call-start = ((), (), s32[]{:S(2)}) async-start(), calls=%async_computation.35 | async-start | bytes 294912
  2447.8 298.1 %reduce-scatter.54.cloned.1.call-start = ((), (), s32[]{:S(2)}) async-start(), calls=%async_computation.36 | async-start | bytes 294912
  2450.8 332.3 %reduce-scatter.58.cloned.1.call-start = ((), (), s32[]{:S(2)}) async-start(), calls=%async_computation.38 | async-start | bytes 589824
  2454.3 365.8 %reduce-scatter.38.cloned.1.call-start = ((), (), s32[]{:S(2)}) async-start(), calls=%async_computation.28 | async-start | bytes 589824 | tf_op jit(solution)/shard_map/reduce_scatter | solution.py:564
  2458.1 399.3 %reduce-scatter.40.cloned.1.call-start = ((), (), s32[]{:S(2)}) async-start(), calls=%async_computation.29 | async-start | bytes 589824 | tf_op jit(solution)/shard_map/reduce_scatter | solution.py:567
  2461.4 433.7 %reduce-scatter.36.cloned.1.call-start = ((), (), s32[]{:S(2)}) async-start(), calls=%async_computation.27 | async-start | bytes 589824 | tf_op jit(solution)/shard_map/reduce_scatter | solution.py:561
  2471.5 460.5 %reduce-scatter.46.cloned.1.call-start = ((), (), s32[]{:S(2)}) async-start(), calls=%async_computation.32 | async-start | bytes 294912 | tf_op jit(solution)/shard_map/reduce_scatter | solution.py:585
  2494.3 483.4 %reduce-scatter.34.cloned.1.call-start = ((), (), s32[]{:S(2)}) async-start(), calls=%async_computation.26 | async-start | bytes 2621440 | tf_op jit(solution)/shard_map/reduce_scatter | solution.py:205
  (160 other events, 7071.0 us)
Sparse Core Ops, SparseCore 0:
  12.3 48.3 all-gather.7
  936.4 53.7 reduce-scatter.27
  994.1 44.8 all-gather.9
  1040.8 26.5 all-gather.11
  1068.8 45.6 all-gather.15
  1116.2 26.8 all-gather.13
  1158.3 46.2 reduce-scatter.31
  1206.9 42.8 reduce-scatter.29
  1254.3 44.8 all-gather.17
  2395.6 46.0 all-reduce.12
  2444.9 40.6 reduce-scatter.59
  2488.8 41.1 reduce-scatter.49
  2533.5 31.3 reduce-scatter.43
  2568.3 31.3 reduce-scatter.41
  2602.6 33.5 reduce-scatter.47
  2639.0 33.6 reduce-scatter.55
  2675.6 33.6 reduce-scatter.51
  2712.2 33.6 reduce-scatter.53
  2749.0 34.0 reduce-scatter.57
  2786.0 34.0 reduce-scatter.37
  2823.2 34.0 reduce-scatter.39
  2861.0 34.0 reduce-scatter.35
  2898.2 33.7 reduce-scatter.45
  2934.1 43.5 reduce-scatter.33
where the time goes:
time: 3050 us; the launch traced here: 3030 us
  other arithmetic  914 us (30%)
  matrix products  861 us (28%)
  waiting for transfers between devices  784 us (26%)
  local copies, waits for them, and re-layouts  215 us (7%)
  blocking collectives  189 us (6%)
  starting transfers between devices  46.3 us (2%)
    another operation x128, other arithmetic, one_block(): lax.linalg.triangular_solve(unit_matrix - pull_write, pull_rhs, left_side...  669 us
    reduce_scatter x4, waiting for transfers between devices, collect_rows(): lax.psum_scatter(partial_value.astype(jnp.bfloat16), 'head', scatter_dime...  181 us
    unnamed x29, waiting for transfers between devices  143 us
    all_gather x4, waiting for transfers between devices, spread_rows(): return lax.all_gather(block_rows, 'head', axis=0, tiled=True)  127 us
    dot_general x48, matrix products, one_block(): jnp.einsum('hck,hdk->hcd', read_left, write_right, precision=HIGHEST)  81.5 us
    dynamic_update_slice x48, other arithmetic, recurrence_blocks(): last_state, emitted_tokens = lax.scan(one_block, start, inputs)  76.7 us
    dot_general x48, matrix products, one_block(): jnp.einsum('hck,hdk->hcd', read_left, key_right, precision=HIGHEST) * within  71.2 us
    dot_general x48, matrix products, one_block(): jnp.einsum('hck,hdk->hcd', pull_left, key_right, precision=HIGHEST) * strict  70.1 us
  transfers between devices with their start and end apart: 42, of which 37 were waited for; matrix products, arithmetic and copies ran while one was open for 4% of the time, Pallas kernels for 0%

commit v1 on v0

v1 whole, which is shorter than its diff:
```python
import functools

import jax
import jax.numpy as jnp
from jax import lax
from jax.experimental import pallas as pl
from jax.experimental.pallas import tpu as pltpu
from jax.sharding import PartitionSpec as P

WIDTH = 64
BLOCK = 64
PAIR = 2 * WIDTH
HIGHEST = lax.Precision.HIGHEST
NN = (((1,), (0,)), ((), ()))
NT = (((1,), (1,)), ((), ()))
TN = (((0,), (0,)), ((), ()))
F32 = jnp.float32
BF16 = jnp.bfloat16
PASSES = 3
GROUP = 4


def mm(left, right, dims, passes=PASSES):
    left_high = left.astype(BF16)
    right_high = right.astype(BF16)

    def dot(a, b):
        return lax.dot_general(a, b, dims, preferred_element_type=F32)

    out = dot(left_high, right_high)
    if passes >= 2:
        out = out + dot((left - left_high.astype(F32)).astype(BF16), right_high)
    if passes >= 3:
        out = out + dot(left_high, (right - right_high.astype(F32)).astype(BF16))
    return out


def iotas(n):
    return lax.broadcasted_iota(jnp.int32, (n, n), 0), lax.broadcasted_iota(jnp.int32, (n, n), 1)


def stack_pair(x):
    lane = lax.broadcasted_iota(jnp.int32, x.shape, 1)
    return jnp.concatenate(
        [jnp.where(lane < WIDTH, x, 0.0), jnp.where(lane < WIDTH, 0.0, x)], axis=0
    )


def join_pair(x):
    half = x.shape[0] // 2
    return x[:half] + x[half:]


def running_sum(x, reverse=False):
    row, col = iotas(BLOCK)
    ones = jnp.where((row <= col) if reverse else (row >= col), 1.0, 0.0).astype(BF16)
    high = x.astype(BF16)
    rest = x - high.astype(F32)
    middle = rest.astype(BF16)
    low = (rest - middle.astype(F32)).astype(BF16)

    def dot(part):
        return lax.dot_general(ones, part, NN, preferred_element_type=F32)

    return dot(high) + dot(middle) + dot(low)


def factors(recept, log_decay, removal, rate, key):
    total = running_sum(log_decay)
    before = total - log_decay
    end = total[BLOCK - 1 : BLOCK]
    grow = jnp.exp(-total)
    fade = jnp.exp(end - total)
    decay = jnp.exp(total)
    decay_before = jnp.exp(before)
    write = removal * rate
    return dict(
        A=-removal * decay_before,
        B=write * grow,
        K=key * grow,
        R=recept * decay,
        BF=write * fade,
        KF=key * fade,
        decay=decay,
        decay_before=decay_before,
        grow=grow,
        fade=fade,
        end=jnp.exp(end),
        write=write,
    )


def causal_mask():
    row, col = iotas(2 * PAIR)
    same = ((row >> 6) & 1) == ((col >> 6) & 1)
    limit = jnp.where(row < PAIR, (row & 63) - 1, row & 63)
    return same & ((col & 63) <= limit)


def triangle_inverses(mats):
    row, col = iotas(PAIR)
    eye = jnp.where(row == col, 1.0, 0.0)
    outs = [eye + jnp.where((row >> 1) == (col >> 1), m, 0.0) for m in mats]
    for level in range(1, 6):
        pick = ((row >> (level + 1)) == (col >> (level + 1))) & ((row >> level) != (col >> level))
        steps = [mm(jnp.where(pick, m, 0.0), x, NN) for m, x in zip(mats, outs)]
        outs = [x + mm(x, s, NN) for x, s in zip(outs, steps)]
    return outs


def forward_kernel(
    group, recept, log_decay, removal, rate, key, val,
    query, local, pairs, inverse, pull, pulled, mapped, transfer, prefix, ending, carry,
):
    sides = recept.shape[1] // PAIR
    row, col = iotas(PAIR)
    eye = jnp.where(row == col, 1.0, 0.0)

    @pl.when(pl.program_id(0) == 0)
    def _():
        for p in range(sides):
            carry[p] = jnp.concatenate([eye, jnp.zeros((PAIR, PAIR), F32)], axis=0)

    mask = causal_mask()
    units = [(j, p) for j in range(group) for p in range(sides)]
    facs, scores, firsts = [], [], []
    for j, p in units:
        rows, lanes = slice(BLOCK * j, BLOCK * j + BLOCK), slice(PAIR * p, PAIR * p + PAIR)
        f = factors(
            recept[rows, lanes], log_decay[rows, lanes], removal[rows, lanes],
            rate[rows, lanes], key[rows, lanes],
        )
        f = {n: (v if n == "end" else stack_pair(v)) for n, v in f.items()
             if n in ("A", "B", "K", "R", "BF", "KF", "end")}
        f["V"] = stack_pair(val[rows, lanes])
        e = mm(
            jnp.concatenate([f["A"], f["R"]], axis=0), jnp.concatenate([f["B"], f["K"]], axis=0), NT
        )
        e = jnp.where(mask, e, 0.0)
        pairs[j, p] = e.astype(pairs.dtype)
        facs.append(f)
        scores.append(e)
        firsts.append(mm(e[:, PAIR:], f["V"], NN))
    inverses = triangle_inverses([e[:PAIR, :PAIR] for e in scores])
    wus = [
        mm(x, jnp.concatenate([f["A"], n[:PAIR]], axis=1), NN)
        for x, f, n in zip(inverses, facs, firsts)
    ]
    reads = [mm(e[PAIR:, :PAIR], wu, NN) for e, wu in zip(scores, wus)]
    writes = [mm(wu, f["BF"], TN) for wu, f in zip(wus, facs)]
    adds = [mm(f["V"], f["KF"], TN) for f in facs]
    state = [carry[p] for p in range(sides)]
    for (j, p), f, x, wu, n, read, wrote, add in zip(
        units, facs, inverses, wus, firsts, reads, writes, adds
    ):
        rows, lanes = slice(BLOCK * j, BLOCK * j + BLOCK), slice(PAIR * p, PAIR * p + PAIR)
        mapping = f["R"] + read[:, :PAIR]
        step = jnp.where(row == col, jnp.broadcast_to(f["end"], (PAIR, PAIR)), 0.0) + wrote[:PAIR]
        both = mm(mapping, state[p], NT)
        query[rows, lanes] = join_pair(both[:, :PAIR])
        local[rows, lanes] = join_pair(both[:, PAIR:] + read[:, PAIR:] + n[PAIR:])
        inverse[j, p] = x.astype(inverse.dtype)
        pull[j, p] = wu[:, :PAIR].astype(pull.dtype)
        pulled[j, p] = wu[:, PAIR:].astype(pulled.dtype)
        mapped[j, p] = mapping.astype(mapped.dtype)
        transfer[j, p] = step.astype(transfer.dtype)
        prefix[j, p] = state[p].astype(prefix.dtype)
        moved = mm(state[p], step, NN)
        state[p] = jnp.concatenate([moved[:PAIR], moved[PAIR:] + wrote[PAIR:] + add], axis=0)
    for p in range(sides):
        carry[p] = state[p]
        ending[p, 0] = join_pair(state[p][:PAIR])
        ending[p, 1] = join_pair(state[p][PAIR:])


def core_forward(recept, log_decay, removal, rate, key, val):
    tokens, wide = recept.shape
    sides = wide // PAIR
    blocks = tokens // BLOCK
    row_spec = pl.BlockSpec((GROUP * BLOCK, wide), lambda i: (i, 0))

    def spec(a, b):
        return pl.BlockSpec((GROUP, sides, a, b), lambda i: (i, 0, 0, 0))

    def kept(a, b):
        return jax.ShapeDtypeStruct((blocks, sides, a, b), F32)

    outs = pl.pallas_call(
        functools.partial(forward_kernel, GROUP),
        grid=(blocks // GROUP,),
        in_specs=[row_spec] * 6,
        out_specs=[row_spec, row_spec, spec(2 * PAIR, 2 * PAIR)]
        + [spec(PAIR, PAIR)] * 5
        + [spec(2 * PAIR, PAIR), pl.BlockSpec((sides, 2, WIDTH, PAIR), lambda i: (0, 0, 0, 0))],
        out_shape=[jax.ShapeDtypeStruct((tokens, wide), F32)] * 2
        + [kept(2 * PAIR, 2 * PAIR)]
        + [kept(PAIR, PAIR)] * 5
        + [kept(2 * PAIR, PAIR), jax.ShapeDtypeStruct((sides, 2, WIDTH, PAIR), F32)],
        scratch_shapes=[pltpu.VMEM((sides, 2 * PAIR, PAIR), F32)],
        cost_estimate=pl.CostEstimate(
            flops=blocks * 1000 * PAIR**3,
            bytes_accessed=blocks * PAIR * PAIR * 4 * 24,
            transcendentals=tokens * wide * 5,
        ),
        name="core_forward",
    )(recept, log_decay, removal, rate, key, val)
    return outs[0], outs[1], outs[2:9], outs[9]


def combine_kernel(position, gathered, query, local, emitted, entering):
    for p in range(query.shape[1] // PAIR):

        def step(s, state):
            return mm(state, stack_pair(gathered[s, p, 0].astype(F32)), NN) + stack_pair(
                gathered[s, p, 1].astype(F32)
            )

        state = lax.fori_loop(0, position[0], step, jnp.zeros((PAIR, PAIR), F32))
        entering[p] = join_pair(state)
        lanes = slice(PAIR * p, PAIR * p + PAIR)
        emitted[:, lanes] = mm(query[:, lanes], state, NT) + local[:, lanes]


def combine(position, gathered, query, local):
    vmem = pl.BlockSpec(memory_space=pltpu.VMEM)
    return pl.pallas_call(
        combine_kernel,
        in_specs=[pl.BlockSpec(memory_space=pltpu.SMEM), vmem, vmem, vmem],
        out_specs=[vmem, vmem],
        out_shape=[
            jax.ShapeDtypeStruct(query.shape, F32),
            jax.ShapeDtypeStruct((query.shape[1] // PAIR, WIDTH, PAIR), F32),
        ],
        cost_estimate=pl.CostEstimate(
            flops=16 * PAIR**3 * 40, bytes_accessed=query.size * 12, transcendentals=0
        ),
        name="core_combine",
    )(position, gathered, query, local)


def backward_kernel(
    group, position, gathered, grads, recept, log_decay, removal, rate, key, val, grad_out,
    pairs, inverse, pull, pulled, mapped, transfer, prefix, entering,
    out_recept, out_decay, out_removal, out_rate, out_key, out_val, carry,
):
    sides = recept.shape[1] // PAIR

    @pl.when(pl.program_id(0) == 0)
    def _():
        last = gathered.shape[0] - 1
        for p in range(sides):

            def step(s, state):
                return mm(state, stack_pair(gathered[last - s, p, 0].astype(F32)), NT) + stack_pair(
                    grads[last - s, p].astype(F32)
                )

            carry[p] = lax.fori_loop(0, last - position[0], step, jnp.zeros((PAIR, PAIR), F32))

    mask = causal_mask()
    states = [carry[p] for p in range(sides)]
    begin = [stack_pair(entering[p]) for p in range(sides)]
    for j in reversed(range(group)):
        for p in range(sides):
            rows, lanes = slice(BLOCK * j, BLOCK * j + BLOCK), slice(PAIR * p, PAIR * p + PAIR)
            key_in, rate_in, removal_in = key[rows, lanes], rate[rows, lanes], removal[rows, lanes]
            f = factors(recept[rows, lanes], log_decay[rows, lanes], removal_in, rate_in, key_in)
            a, b, k, r, bf, kf = (stack_pair(f[n]) for n in ("A", "B", "K", "R", "BF", "KF"))
            v, go = stack_pair(val[rows, lanes]), stack_pair(grad_out[rows, lanes])
            g = states[p]
            e = pairs[j, p].astype(F32)
            pre = prefix[j, p].astype(F32)
            state = mm(begin[p], pre[:PAIR], NN) + pre[PAIR:]
            u = mm(pull[j, p].astype(F32), state, NT) + pulled[j, p].astype(F32)
            through = mm(jnp.concatenate([bf, kf], axis=0), g, NT)
            grad_u = mm(e[PAIR:, :PAIR], go, TN) + through[:PAIR]
            z = mm(inverse[j, p].astype(F32), grad_u, TN)
            zo = jnp.concatenate([z, go], axis=0)
            uv = jnp.concatenate([u, v], axis=0)
            d = jnp.where(mask, mm(zo, uv, NT), 0.0)
            left = mm(d, jnp.concatenate([b, k], axis=0), NN) + mm(zo, state, NN)
            right = mm(d, jnp.concatenate([a, r], axis=0), TN)
            grad_v = mm(e[:, PAIR:], zo, TN) + through[PAIR:]
            out = mm(uv, g, NN)
            states[p] = mm(g, transfer[j, p].astype(F32), NT) + mm(
                go, mapped[j, p].astype(F32), TN
            )
            grad_a, grad_r = join_pair(left[:PAIR]), join_pair(left[PAIR:])
            grad_b, grad_k = join_pair(right[:PAIR]), join_pair(right[PAIR:])
            grad_bf, grad_kf = join_pair(out[:PAIR]), join_pair(out[PAIR:])
            to_write = f["grow"] * grad_b + f["fade"] * grad_bf
            to_key = f["grow"] * grad_k + f["fade"] * grad_kf
            to_end = jnp.sum(
                f["BF"] * grad_bf + f["KF"] * grad_kf, axis=0, keepdims=True
            ) + f["end"] * jnp.sum(state * g, axis=0, keepdims=True)
            to_before = f["A"] * grad_a
            to_sum = f["R"] * grad_r - f["write"] * to_write - key_in * to_key + to_before
            out_recept[rows, lanes] = f["decay"] * grad_r
            out_decay[rows, lanes] = running_sum(to_sum, True) - to_before + to_end
            out_removal[rows, lanes] = rate_in * to_write - f["decay_before"] * grad_a
            out_rate[rows, lanes] = removal_in * to_write
            out_key[rows, lanes] = to_key
            out_val[rows, lanes] = join_pair(grad_v)
    for p in range(sides):
        carry[p] = states[p]


def core_backward(position, gathered, grads, operands, grad_out, saved, entering):
    tokens, wide = grad_out.shape
    sides = wide // PAIR
    blocks = tokens // BLOCK
    group = 2
    steps = blocks // group
    row_spec = pl.BlockSpec((group * BLOCK, wide), lambda i: (steps - 1 - i, 0))

    def spec(kept):
        return pl.BlockSpec((group,) + kept.shape[1:], lambda i: (steps - 1 - i, 0, 0, 0))

    vmem = pl.BlockSpec(memory_space=pltpu.VMEM)
    return pl.pallas_call(
        functools.partial(backward_kernel, group),
        grid=(steps,),
        in_specs=[pl.BlockSpec(memory_space=pltpu.SMEM), vmem, vmem]
        + [row_spec] * 7
        + [spec(kept) for kept in saved]
        + [vmem],
        out_specs=[row_spec] * 6,
        out_shape=[jax.ShapeDtypeStruct((tokens, wide), F32)] * 6,
        scratch_shapes=[pltpu.VMEM((sides, PAIR, PAIR), F32)],
        cost_estimate=pl.CostEstimate(
            flops=blocks * 800 * PAIR**3,
            bytes_accessed=blocks * PAIR * PAIR * 4 * 30,
            transcendentals=tokens * wide * 5,
        ),
        name="core_backward",
    )(position, gathered, grads, *operands, grad_out, *saved, entering)


def shifted(block, axis, distance):
    devices = range(lax.axis_size(axis))
    route = [(i - distance, i) for i in devices if i - distance in devices]
    return lax.ppermute(block, axis, route)


def product(left, right):
    return jnp.dot(left, right, preferred_element_type=F32)


def cross_rows(left, right):
    return lax.dot_general(left, right, TN, preferred_element_type=F32)


def cross_cols(left, right):
    return lax.dot_general(left, right, NT, preferred_element_type=F32)


def layer_norm(content_tokens, norm_gain, norm_bias):
    row_mean = jnp.mean(content_tokens, axis=-1, keepdims=True)
    centred = content_tokens - row_mean
    row_var = jnp.mean(centred * centred, axis=-1, keepdims=True)
    return centred * lax.rsqrt(row_var + 1e-05) * norm_gain + norm_bias


def head_sum(x):
    row, col = iotas(x.shape[-1])
    ones = jnp.where(row // WIDTH == col // WIDTH, 1.0, 0.0)
    return jnp.dot(x, ones, precision=HIGHEST, preferred_element_type=F32)


def prepare(
    acceptor_tokens,
    key_base,
    value_base,
    decay_prod,
    rate_prod,
    blend_prod,
    earliest_block_vals,
    fading_baseline,
    stepsize_baseline,
    residual_blend_baseline,
    erasing_address_factor,
    address_rate_portion,
):
    log_decay = -jnp.exp(-jax.nn.softplus(-(fading_baseline + decay_prod)) - 0.5)
    rate_vals = jax.nn.sigmoid(stepsize_baseline + rate_prod)
    blend_vals = jax.nn.sigmoid(residual_blend_baseline + blend_prod)
    content_tokens = value_base + (earliest_block_vals - value_base) * blend_vals
    removal = key_base * erasing_address_factor
    removal = removal * lax.rsqrt(head_sum(removal * removal) + 1e-06)
    address_signals = key_base * (1.0 + (rate_vals - 1.0) * address_rate_portion)
    return (acceptor_tokens, log_decay, removal, rate_vals, address_signals, content_tokens)


def wrap_around_rule(
    emitted_tokens,
    acceptor_tokens,
    address_signals,
    content_tokens,
    sigmoid_valve_levels,
    present_extra_factor,
    attend_standardize_factor,
    attend_standardize_shift,
):
    centred = emitted_tokens - head_sum(emitted_tokens) * (1.0 / WIDTH)
    head_var = head_sum(centred * centred) * (1.0 / WIDTH)
    per_attend_split = (
        centred * lax.rsqrt(head_var + 0.00064) * attend_standardize_factor
        + attend_standardize_shift
    )
    present_token_extra = (
        head_sum(acceptor_tokens * address_signals * present_extra_factor) * content_tokens
    )
    return (per_attend_split + present_token_extra) * sigmoid_valve_levels


def spread_rows(block_rows):
    return lax.all_gather(block_rows, "head", axis=0, tiled=True)


def collect_rows(partial_value):
    return lax.psum_scatter(
        partial_value.astype(BF16), "head", scatter_dimension=0, tiled=True
    ).astype(F32)


def with_before(token_rows):
    arriving = shifted(token_rows[-1:], "seq", 1)
    return jnp.concatenate([arriving, token_rows[:-1]], axis=0)


def fold_before(grad_rows, grad_before):
    arriving = shifted(grad_before[:1], "seq", -1)
    return grad_rows + jnp.concatenate([grad_before[1:], arriving], axis=0)


def sum_over(part, axis):
    return jnp.sum(lax.all_gather(part, axis, axis=0), axis=0)


def scatter_sum(part, axis):
    count = lax.axis_size(axis)
    pieces = part.astype(BF16).reshape((count, part.shape[0] // count) + part.shape[1:])
    pieces = lax.all_to_all(pieces, axis, split_axis=0, concat_axis=0)
    return jnp.sum(pieces.astype(F32), axis=0)


def columns(whole, widths):
    pieces, at = [], 0
    for width in widths:
        pieces.append(whole[:, at : at + width])
        at += width
    return pieces


def body(
    incoming_hidden,
    earliest_block_vals,
    upstream_sensitivity,
    opening_standardize_factor,
    opening_standardize_shift,
    attention_lag_blend,
    acceptor_linear_map,
    address_linear_map,
    content_linear_map,
    fading_narrowing,
    fading_widening,
    fading_baseline,
    stepsize_narrowing,
    stepsize_widening,
    stepsize_baseline,
    residual_blend_narrowing,
    residual_blend_widening,
    residual_blend_baseline,
    valve_narrowing,
    valve_widening,
    erasing_address_factor,
    address_rate_portion,
    present_extra_factor,
    attend_standardize_factor,
    attend_standardize_shift,
    emitted_linear_map,
    closing_standardize_factor,
    closing_standardize_shift,
    feedforward_lag_blend,
    feedforward_entrance,
    feedforward_exit,
):
    position = lax.axis_index("seq").astype(jnp.int32).reshape(1)
    early = [
        acceptor_linear_map,
        address_linear_map,
        content_linear_map,
        fading_narrowing,
        stepsize_narrowing,
        residual_blend_narrowing,
        valve_narrowing,
    ]
    early_widths = [part.shape[1] for part in early]
    wideners = [fading_widening, stepsize_widening, residual_blend_widening, valve_widening]
    widener_rows = [part.shape[0] for part in wideners]
    late = [emitted_linear_map.T, feedforward_entrance, feedforward_exit.T]
    late_widths = [part.shape[1] for part in late]
    residual_in = incoming_hidden.astype(F32)
    normed_front, front_back = jax.vjp(
        layer_norm, residual_in, opening_standardize_factor, opening_standardize_shift
    )
    normed = spread_rows(normed_front.astype(BF16))
    early_full = lax.all_gather(jnp.concatenate(early, axis=1), "seq", axis=0, tiled=True)
    (
        full_recept,
        full_key,
        full_value,
        full_decay_down,
        full_rate_down,
        full_blend_down,
        full_gate_down,
    ) = columns(early_full, early_widths)
    wide_full = lax.all_gather(jnp.concatenate(wideners, axis=0), "seq", axis=0)
    ups, at = [], 0
    for count in widener_rows:
        ups.append(wide_full[:, at : at + count].reshape(-1, wide_full.shape[-1]))
        at += count
    full_decay_up, full_rate_up, full_blend_up, full_gate_up = ups
    late_full = lax.all_gather(jnp.concatenate(late, axis=1), "seq", axis=0, tiled=True)
    full_output_t, full_channel_key, full_channel_value_t = columns(late_full, late_widths)
    grad_top = spread_rows(upstream_sensitivity)

    normed_wide = normed.astype(F32)
    shift_delta = with_before(normed).astype(F32) - normed_wide
    mixed_in = [
        (normed_wide + shift_delta * attention_lag_blend[p][None]).astype(BF16) for p in range(6)
    ]
    acceptor_tokens = product(mixed_in[0], full_recept)
    key_base = product(mixed_in[2], full_key)
    value_base = product(mixed_in[3], full_value)
    decay_lat = product(mixed_in[1], full_decay_down)
    decay_tanh = jnp.tanh(decay_lat).astype(BF16)
    rate_lat = product(mixed_in[4], full_rate_down).astype(BF16)
    blend_lat = product(mixed_in[3], full_blend_down).astype(BF16)
    gate_pre = product(mixed_in[5], full_gate_down)
    gate_lat = jax.nn.sigmoid(gate_pre).astype(BF16)
    decay_prod = product(decay_tanh, full_decay_up)
    rate_prod = product(rate_lat, full_rate_up)
    blend_prod = product(blend_lat, full_blend_up)
    sigmoid_valve_levels = product(gate_lat, full_gate_up)
    scan_operands, prepare_back = jax.vjp(
        prepare,
        acceptor_tokens,
        key_base,
        value_base,
        decay_prod,
        rate_prod,
        blend_prod,
        earliest_block_vals.astype(F32),
        fading_baseline,
        stepsize_baseline,
        residual_blend_baseline,
        erasing_address_factor,
        address_rate_portion,
    )
    query_map, local_out, saved, ending = core_forward(*scan_operands)
    gathered = lax.all_gather(ending.astype(BF16), "seq", axis=0)
    emitted_tokens, entering = combine(position, gathered, query_map, local_out)
    branch_wide, finish_back = jax.vjp(
        wrap_around_rule,
        emitted_tokens,
        scan_operands[0],
        scan_operands[4],
        scan_operands[5],
        sigmoid_valve_levels,
        present_extra_factor,
        attend_standardize_factor,
        attend_standardize_shift,
    )
    auxiliary_path = branch_wide.astype(BF16)
    middle = residual_in + collect_rows(cross_cols(auxiliary_path, full_output_t))
    normed_mid_front, middle_back = jax.vjp(
        layer_norm, middle, closing_standardize_factor, closing_standardize_shift
    )
    normed_mid = spread_rows(normed_mid_front.astype(BF16))
    mid_wide = normed_mid.astype(F32)
    mid_delta = with_before(normed_mid).astype(F32) - mid_wide
    keyed_in = (mid_wide + mid_delta * feedforward_lag_blend).astype(BF16)
    hidden_pre = product(keyed_in, full_channel_key)
    hidden = jnp.square(jax.nn.relu(hidden_pre)).astype(BF16)
    grad_pre = (product(grad_top, full_channel_value_t) * 2.0 * jax.nn.relu(hidden_pre)).astype(
        BF16
    )
    grad_keyed = cross_cols(grad_pre, full_channel_key)
    feedforward_lag_blend_adjoint = jnp.sum(grad_keyed * mid_delta, axis=0)
    grad_mid_rows = fold_before(
        grad_keyed * (1.0 - feedforward_lag_blend), grad_keyed * feedforward_lag_blend
    )
    grad_middle_in, closing_standardize_factor_adj, closing_standardize_shift_adj = middle_back(
        collect_rows(grad_mid_rows)
    )
    grad_middle = upstream_sensitivity.astype(F32) + grad_middle_in
    grad_attend = spread_rows(grad_middle.astype(BF16))
    result = middle + collect_rows(cross_cols(hidden, full_channel_value_t))
    late_grads = lax.psum_scatter(
        jnp.concatenate(
            [
                cross_rows(grad_attend, auxiliary_path).astype(BF16),
                cross_rows(keyed_in, grad_pre).astype(BF16),
                cross_rows(grad_top, hidden).astype(BF16),
            ],
            axis=1,
        ),
        "seq",
        scatter_dimension=0,
        tiled=True,
    ).astype(F32)
    emitted_t, feedforward_entrance_adjoint, exit_t = columns(late_grads, late_widths)
    emitted_linear_map_adjoint = emitted_t.T
    feedforward_exit_adjoint = exit_t.T
    grad_branch = product(grad_attend, full_output_t)
    (
        grad_outputs,
        grad_recept_extra,
        grad_keys_extra,
        grad_values_extra,
        grad_gate_vals,
        present_extra_adjoint,
        attend_standardize_factor_adj,
        attend_standardize_shift_adj,
    ) = finish_back(grad_branch)
    row, col = iotas(PAIR)
    same_head = (row // WIDTH) == (col // WIDTH)
    grad_local = []
    for p in range(query_map.shape[1] // PAIR):
        lanes = slice(PAIR * p, PAIR * p + PAIR)
        square = lax.dot_general(
            grad_outputs[:, lanes],
            query_map[:, lanes],
            TN,
            precision=HIGHEST,
            preferred_element_type=F32,
        )
        grad_local.append(join_pair(jnp.where(same_head, square, 0.0)))
    grads = lax.all_gather(jnp.stack(grad_local).astype(BF16), "seq", axis=0)
    grad_kernel = core_backward(
        position, gathered, grads, scan_operands, grad_outputs, saved, entering
    )
    grad_kernel = (
        grad_kernel[0] + grad_recept_extra,
        grad_kernel[1],
        grad_kernel[2],
        grad_kernel[3],
        grad_kernel[4] + grad_keys_extra,
        grad_kernel[5] + grad_values_extra,
    )
    (
        grad_recept,
        grad_key_base,
        grad_value_base,
        grad_decay_prod,
        grad_rate_prod,
        grad_blend_prod,
        earliest_block_vals_adjoint,
        fading_baseline_adjoint,
        stepsize_baseline_adjoint,
        residual_blend_baseline_adj,
        erasing_address_factor_adj,
        address_rate_portion_adjoint,
    ) = prepare_back(grad_kernel)
    recept_back = grad_recept.astype(BF16)
    key_back = grad_key_base.astype(BF16)
    value_back = grad_value_base.astype(BF16)
    decay_prod_back = grad_decay_prod.astype(BF16)
    rate_prod_back = grad_rate_prod.astype(BF16)
    blend_prod_back = grad_blend_prod.astype(BF16)
    gate_back = grad_gate_vals.astype(BF16)
    tanh_wide = jnp.tanh(decay_lat)
    gate_sigmoid = jax.nn.sigmoid(gate_pre)
    decay_lat_back = (
        cross_cols(decay_prod_back, full_decay_up) * (1.0 - tanh_wide * tanh_wide)
    ).astype(BF16)
    rate_lat_back = cross_cols(rate_prod_back, full_rate_up).astype(BF16)
    blend_lat_back = cross_cols(blend_prod_back, full_blend_up).astype(BF16)
    gate_pre_back = (
        cross_cols(gate_back, full_gate_up) * gate_sigmoid * (1.0 - gate_sigmoid)
    ).astype(BF16)
    grad_mixed = [
        cross_cols(recept_back, full_recept),
        cross_cols(decay_lat_back, full_decay_down),
        cross_cols(key_back, full_key),
        cross_cols(value_back, full_value) + cross_cols(blend_lat_back, full_blend_down),
        cross_cols(rate_lat_back, full_rate_down),
        cross_cols(gate_pre_back, full_gate_down),
    ]
    shift_sums = jnp.stack([jnp.sum(g * shift_delta, axis=0) for g in grad_mixed])
    plain = sum(grad_mixed)
    lagged = sum(g * attention_lag_blend[p][None] for p, g in enumerate(grad_mixed))
    grad_normed = fold_before(plain - lagged, lagged)
    grad_front_in, opening_standardize_factor_adj, opening_standardize_shift_adj = front_back(
        collect_rows(grad_normed)
    )
    incoming_hidden_adjoint = grad_middle + grad_front_in
    early_grads = scatter_sum(
        jnp.concatenate(
            [
                cross_rows(mixed_in[0], recept_back).astype(BF16),
                cross_rows(mixed_in[2], key_back).astype(BF16),
                cross_rows(mixed_in[3], value_back).astype(BF16),
                cross_rows(mixed_in[1], decay_lat_back).astype(BF16),
                cross_rows(mixed_in[4], rate_lat_back).astype(BF16),
                cross_rows(mixed_in[3], blend_lat_back).astype(BF16),
                cross_rows(mixed_in[5], gate_pre_back).astype(BF16),
            ],
            axis=1,
        ),
        "seq",
    )
    (
        acceptor_linear_map_adjoint,
        address_linear_map_adjoint,
        content_linear_map_adjoint,
    ) = columns(early_grads, early_widths[:3])
    narrow = early_grads[:, sum(early_widths[:3]) :]
    narrow = sum_over(narrow.astype(BF16), "head").astype(F32)
    (
        fading_narrowing_adjoint,
        stepsize_narrowing_adjoint,
        residual_blend_narrowing_adj,
        valve_narrowing_adjoint,
    ) = columns(narrow, early_widths[3:])
    count = lax.axis_size("seq")
    up_parts = [
        cross_rows(lat, back).astype(BF16).reshape(count, rows, -1)
        for lat, back, rows in zip(
            (decay_tanh, rate_lat, blend_lat, gate_lat),
            (decay_prod_back, rate_prod_back, blend_prod_back, gate_back),
            widener_rows,
        )
    ]
    up_sum = lax.all_to_all(jnp.concatenate(up_parts, axis=1), "seq", split_axis=0, concat_axis=0)
    up_sum = jnp.sum(up_sum.astype(F32), axis=0)
    up_grads, at = [], 0
    for rows in widener_rows:
        up_grads.append(up_sum[at : at + rows])
        at += rows
    (
        fading_widening_adjoint,
        stepsize_widening_adjoint,
        residual_blend_widening_adj,
        valve_widening_adjoint,
    ) = up_grads
    everywhere = jnp.concatenate(
        [
            shift_sums,
            jnp.stack(
                [
                    opening_standardize_factor_adj,
                    opening_standardize_shift_adj,
                    closing_standardize_factor_adj,
                    closing_standardize_shift_adj,
                    feedforward_lag_blend_adjoint,
                ]
            ),
        ],
        axis=0,
    )
    everywhere = sum_over(everywhere, "head")
    head_vectors = jnp.stack(
        [
            fading_baseline_adjoint,
            stepsize_baseline_adjoint,
            residual_blend_baseline_adj,
            erasing_address_factor_adj,
            address_rate_portion_adjoint,
            present_extra_adjoint,
            attend_standardize_factor_adj,
            attend_standardize_shift_adj,
        ]
    )
    vectors = sum_over(jnp.concatenate([everywhere.reshape(-1), head_vectors.reshape(-1)]), "seq")
    split = everywhere.size
    everywhere = vectors[:split].reshape(everywhere.shape)
    head_vectors = vectors[split:].reshape(head_vectors.shape)
    shift_sums = everywhere[:6]
    return (
        result.astype(BF16),
        incoming_hidden_adjoint,
        earliest_block_vals_adjoint,
        everywhere[6],
        everywhere[7],
        jnp.concatenate([shift_sums[:1], shift_sums[2:]], axis=0),
        shift_sums[1],
        acceptor_linear_map_adjoint,
        address_linear_map_adjoint,
        content_linear_map_adjoint,
        fading_narrowing_adjoint,
        fading_widening_adjoint,
        head_vectors[0],
        stepsize_narrowing_adjoint,
        stepsize_widening_adjoint,
        head_vectors[1],
        residual_blend_narrowing_adj,
        residual_blend_widening_adj,
        head_vectors[2],
        valve_narrowing_adjoint,
        valve_widening_adjoint,
        head_vectors[3],
        head_vectors[4],
        head_vectors[5],
        head_vectors[6],
        head_vectors[7],
        emitted_linear_map_adjoint,
        everywhere[8],
        everywhere[9],
        everywhere[10],
        feedforward_entrance_adjoint,
        feedforward_exit_adjoint,
    )


def solution(mesh):
    in_specs = (
        P(("seq", "head"), None),
        P("seq", "head"),
        P(("seq", "head"), None),
        P(),
        P(),
        P(),
        P("seq", "head"),
        P("seq", "head"),
        P("seq", "head"),
        P("seq", None),
        P("seq", "head"),
        P("head"),
        P("seq", None),
        P("seq", "head"),
        P("head"),
        P("seq", None),
        P("seq", "head"),
        P("head"),
        P("seq", None),
        P("seq", "head"),
        P("head"),
        P("head"),
        P("head"),
        P("head"),
        P("head"),
        P("head", "seq"),
        P(),
        P(),
        P(),
        P("seq", "head"),
        P("head", "seq"),
    )
    out_specs = (
        P(("seq", "head"), None),
        P(("seq", "head"), None),
        P("seq", "head"),
        P(),
        P(),
        P(),
        P(),
        P("seq", "head"),
        P("seq", "head"),
        P("seq", "head"),
        P("seq", None),
        P("seq", "head"),
        P("head"),
        P("seq", None),
        P("seq", "head"),
        P("head"),
        P("seq", None),
        P("seq", "head"),
        P("head"),
        P("seq", None),
        P("seq", "head"),
        P("head"),
        P("head"),
        P("head"),
        P("head"),
        P("head"),
        P("head", "seq"),
        P(),
        P(),
        P(),
        P("seq", "head"),
        P("head", "seq"),
    )
    return jax.shard_map(body, mesh=mesh, in_specs=in_specs, out_specs=out_specs, check_vma=False)
```

time: 3050 us -> 746 us (0.24)
  other arithmetic: 914 us -> 49.6 us
  matrix products: 861 us -> 113 us
  waiting for transfers between devices: 784 us -> 335 us
  local copies, waits for them, and re-layouts: 215 us -> 36.7 us
  blocking collectives: 189 us -> 66.8 us
  Pallas kernels: 0 us -> 102 us
  starting transfers between devices: 46.3 us -> 15.4 us
    dot_general x604 -> x52, matrix products: 835 us -> 113 us  [the longest x14 37.2 us: product(): return jnp.dot(left, right, preferred_element_type=F32)]
    another operation x161 -> x3, other arithmetic: 690 us -> 0.02 us  [body(): grads = lax.all_gather(jnp.stack(grad_local).astype(BF16), 'seq', axis=0)]
    reduce_scatter x12 -> x4, waiting for transfers between devices: 398 us -> 126 us  [collect_rows(): lax.psum_scatter(partial_value.astype(BF16), 'head', scatter_dimension=0,...]
    unnamed x29 -> x12, waiting for transfers between devices: 143 us -> 1.1 us
    pallas_call x0 -> x3, Pallas kernels: none -> 102 us  [the longest x1 55.1 us: core_backward(): pl.pallas_call(functools.partial(backward_kernel, group), grid=(steps,),...]
    dynamic_update_slice x48 -> x0, other arithmetic: 76.7 us -> none  [recurrence_blocks(): last_state, emitted_tokens = lax.scan(one_block, start, inputs)]
    psum x2 -> x0, blocking collectives: 54 us -> none  [the longest x1 40.7 us: body(): lax.psum((opening_standardize_factor_adj, opening_standardize_shift_adj,...]
    all_gather x12 -> x6, blocking collectives: 113 us -> 66.8 us  [the longest x3 36.1 us: sum_over(): return jnp.sum(lax.all_gather(part, axis, axis=0), axis=0)]
  transfers between devices with their start and end apart: 42 -> 17, of which waited for: 37 -> 11; matrix products, arithmetic and copies ran while one was open for 4% -> 15% of each run, Pallas kernels for 0% -> 6%
where the time goes in v1:
time: 746 us; the launch traced here: 735 us
  waiting for transfers between devices  335 us (45%)
  matrix products  113 us (15%)
  Pallas kernels  102 us (14%)
  blocking collectives  66.8 us (9%)
  other arithmetic  49.6 us (7%)
  local copies, waits for them, and re-layouts  36.7 us (5%)
  between operations  16.4 us (2%)
  starting transfers between devices  15.4 us (2%)
    all_gather x4, waiting for transfers between devices, spread_rows(): return lax.all_gather(block_rows, 'head', axis=0, tiled=True)  166 us
    reduce_scatter x4, waiting for transfers between devices, collect_rows(): lax.psum_scatter(partial_value.astype(BF16), 'head', scatter_dimension=0,...  126 us
    pallas_call x1, Pallas kernels, core_backward(): pl.pallas_call(functools.partial(backward_kernel, group), grid=(steps,),...  55.1 us
    pallas_call x1, Pallas kernels, core_forward(): pl.pallas_call(functools.partial(forward_kernel, GROUP), grid=(blocks //...  43 us
    dot_general x14, matrix products, product(): return jnp.dot(left, right, preferred_element_type=F32)  37.2 us
    all_gather x3, blocking collectives, sum_over(): return jnp.sum(lax.all_gather(part, axis, axis=0), axis=0)  36.1 us
    dot_general x14, matrix products, cross_cols(): return lax.dot_general(left, right, NT, preferred_element_type=F32)  34.6 us
    all_to_all x1, waiting for transfers between devices, scatter_sum(): pieces = lax.all_to_all(pieces, axis, split_axis=0, concat_axis=0)  26.3 us
  transfers between devices with their start and end apart: 17, of which 11 were waited for; matrix products, arithmetic and copies ran while one was open for 15% of the time, Pallas kernels for 6%

profile of v1, /device:TPU:0, one launch (start us, length us, event | category | flops | bytes accessed | tf_op | source)
XLA Modules:
  0.0 735.0 jit_solution(11879017072984711151)
XLA Ops:
  18.8 41.9 %all-gather.14.cloned.1.call-done = bf16[1024,1024]{1,0:T(8,128)(2,1)} async-done(((bf16[256,1024]{1,0:T(8,128)(2,1)}), bf16[1024,1024]{1,0:T(8,128)(2,1)}) %all-gather.14.cloned.1.call-update) | async-done | bytes 2097168 | tf_op jit(solution)/shard_map/all_gather | solution.py:417
  62.9 9.6 %all-gather.5 = bf16[8,36,256]{2,1,0:T(8,128)(2,1)S(1)} all-gather(bf16[1,36,256]{2,1,0:T(8,128)(2,1)S(1)} %maximum_bitcast_fusion), channel_id=2, replica_groups=mesh['seq'=8,'head'=4] {'seq'}, dimensions={0}, use_global_device_ids=true | all-gather | bytes 165888 | tf_op jit(solution)/shard_map/all_gather | solution.py:518
  72.7 4.7 fusion.5
  77.4 13.5 %all-gather.16.cloned.1.call-done = bf16[1024,1056]{1,0:T(8,128)(2,1)} async-done(((bf16[128,1056]{1,0:T(8,128)(2,1)}), bf16[1024,1056]{1,0:T(8,128)(2,1)}) %all-gather.16.cloned.1.call-update) | async-done | bytes 2162704 | tf_op jit(solution)/shard_map/all_gather | solution.py:508
  107.3 43.0 %core_forward.1 = (f32[1024,256]{1,0:T(8,128)}, f32[1024,256]{1,0:T(8,128)}, f32[16,2,256,256]{3,2,1,0:T(8,128)}, f32[16,2,128,128]{3,2,1,0:T(8,128)}, f32[16,2,...) custom-call(f32[1024,256]{1,0:T(8,128)} %get-tuple-element.267.recep, ...), custom_call_target="tpu_custom_call" | custom-call | flops 33554432000 | bytes 25165824 | tf_op jit(solution)/shard_map/core_forward/pallas_call | solution.py:188
  151.2 10.8 %all-gather.1 = bf16[16,2,64,128]{3,2,1,0:T(8,128)(2,1)} all-gather(bf16[2,2,64,128]{3,2,1,0:T(8,128)(2,1)S(1)} %convert_element_type.216), channel_id=3, replica_groups=mesh['seq'=8,'head'=4] {'seq'}, dimensions={0}, use_global_device_ids=true | all-gather | bytes 589824 | tf_op jit(solution)/shard_map/all_gather | solution.py:562
  162.0 3.6 core_combine.1
  179.4 46.1 %reduce-scatter.8.cloned.1.call-done = bf16[256,1024]{1,0:T(8,128)(2,1)} async-done(((bf16[1024,1024]{1,0:T(8,128)(2,1)}), bf16[256,1024]{1,0:T(8,128)(2,1)}) %reduce-scatter.8.cloned.1.call-update) | async-done | bytes 524304 | tf_op jit(solution)/shard_map/reduce_scatter | solution.py:421
  231.0 44.4 %all-gather.20.cloned.1.call-done = bf16[1024,1024]{1,0:T(8,128)(2,1)} async-done(((bf16[256,1024]{1,0:T(8,128)(2,1)}), bf16[1024,1024]{1,0:T(8,128)(2,1)}) %all-gather.20.cloned.1.call-update) | async-done | bytes 2097168 | tf_op jit(solution)/shard_map/all_gather | solution.py:417
  278.4 7.3 fusion.14
  285.7 35.5 %all-gather.22.cloned.1.call-done = bf16[1024,1024]{1,0:T(8,128)(2,1)} async-done(((bf16[256,1024]{1,0:T(8,128)(2,1)}), bf16[1024,1024]{1,0:T(8,128)(2,1)}) %all-gather.22.cloned.1.call-update) | async-done | bytes 2097168 | tf_op jit(solution)/shard_map/all_gather | solution.py:417
  321.3 6.0 fusion.9
  327.3 5.7 multiply_reduce_fusion
  338.6 6.6 convolution_convert_fusion.1
  345.3 37.3 %reduce-scatter.12.cloned.1.call-done = bf16[256,1024]{1,0:T(8,128)(2,1)} async-done(((bf16[1024,1024]{1,0:T(8,128)(2,1)}), bf16[256,1024]{1,0:T(8,128)(2,1)}) %reduce-scatter.12.cloned.1.call-update) | async-done | bytes 524304 | tf_op jit(solution)/shard_map/reduce_scatter | solution.py:421
  384.7 43.0 %reduce-scatter.10.cloned.1.call-done = bf16[256,1024]{1,0:T(8,128)(2,1)} async-done(((bf16[1024,1024]{1,0:T(8,128)(2,1)}), bf16[256,1024]{1,0:T(8,128)(2,1)}) %reduce-scatter.10.cloned.1.call-update) | async-done | bytes 524304 | tf_op jit(solution)/shard_map/reduce_scatter | solution.py:421
  433.7 44.5 %all-gather.24.cloned.1.call-done = bf16[1024,1024]{1,0:T(8,128)(2,1)} async-done(((bf16[256,1024]{1,0:T(8,128)(2,1)}), bf16[1024,1024]{1,0:T(8,128)(2,1)}) %all-gather.24.cloned.1.call-update) | async-done | bytes 2097168 | tf_op jit(solution)/shard_map/all_gather | solution.py:417
  478.2 4.5 fusion.197
  487.7 10.3 %all_gather.62.grads = bf16[8,2,64,128]{3,2,1,0:T(8,128)(2,1)} all-gather(bf16[1,2,64,128]{3,2,1,0:T(8,128)(2,1)S(1)} %pad_maximum_fusion.6), channel_id=1, replica_groups=mesh['seq'=8,'head'=4] {'seq'}, dimensions={0}, use_global_device_ids=true | all-gather | bytes 294912 | tf_op jit(solution)/shard_map/all_gather | solution.py:640
  498.0 55.1 %core_backward.1 = (f32[1024,256]{1,0:T(8,128)}, f32[1024,256]{1,0:T(8,128)}, f32[1024,256]{1,0:T(8,128)}, f32[1024,256]{1,0:T(8,128)}, f32[1024,256]{1,0:T(8,128)}, /*index=5*/f32[1024,256]{1,0:T(8,128)}) custom-call(s32[1]{0:T(128)} %bitcast.position, bf16[8,2,2,64,128]{4,3,2,1,0:T(8,128)(2,1)} %bitcast.131, bf16[8,2,64,128]{3,2,1,0:T(8,128)(2,1)} %all_gather.62.grads, ...), custom_call_target="tpu_custom_call" | custom-call | flops 26843545600 | bytes 31457280 | tf_op jit(solution)/shard_map/core_backward/pallas_call | solution.py:320
  553.2 4.3 add_add_fusion.1
  574.9 9.7 %multiply_reduce_fusion.1 = (f32[1024]{0:T(1024)}, f32[1024]{0:T(1024)}, f32[1024]{0:T(1024)}, f32[1024]{0:T(1024)}, f32[1024]{0:T(1024)}, /*index=5*/f32[1024]{0:T(1024)}, f32[1024,1024]{1,0:T(8,128)}, f32[1024,1024]{1,0:T(8,128)}) fusion(bf16[1024,1024]{1,0:T(8,128)(2,1)S(1)} %copy-done, bf16[1023,1024]{1,0:T(8,128)(2,1)S(1)} %bitcast.122, ...), kind=kOutput, calls=%fused_computation.25 | convolution fusion | flops 298838016 | bytes 34127872 | tf_op jit(solution)/shard_map/dot_general | solution.py:354
  586.6 5.1 slice.354
  591.8 8.2 %fusion.8 = bf16[1024,1024]{1,0:T(8,128)(2,1)} fusion(f32[1,1024]{1,0:T(1,128)S(1)} %collective-permute-done.3, f32[1023,1024]{1,0:T(8,128)} %slice.354, f32[1024,1024]{1,0:T(8,128)} %get-tuple-element.274, f32[1024,1024]{1,0:T(8,128)S(1)} %fusion.140, f32[1024,1024]{1,0:T(8,128)} %convolution_add_fusion, f32[1024,1024]{1,0:T(8,128)S(1)} %fusion.113, ...), kind=kLoop, calls=%fused_computation.21 | loop fusion | flops 20971520 | bytes 31481856 | tf_op jit(solution)/shard_map/convert_element_type | solution.py:422
  600.0 5.4 convert_bitcast_fusion
  611.3 6.9 copy.111
  625.7 4.0 all-to-all-start.1
  640.5 4.4 all-to-all-start
  647.9 26.3 %all-to-all-done = bf16[8,128,1056]{1,2,0:T(8,128)(2,1)} async-done(((bf16[8,128,1056]{1,2,0:T(8,128)(2,1)}), bf16[8,128,1056]{1,2,0:T(8,128)(2,1)}, u32[]{:S(2)}, u32[]{:S(2)}) %all-to-all-start) | async-done | bytes 2162720 | tf_op jit(solution)/shard_map/all_to_all | solution.py:443
  676.2 13.1 %all-gather.4 = bf16[512,288]{0,1:T(8,128)(2,1)S(1)} all-gather(bf16[128,288]{0,1:T(8,128)(2,1)S(1)} %slice.460), channel_id=6, replica_groups=mesh['seq'=8,'head'=4] {'head'}, dimensions={0}, use_global_device_ids=true | all-gather | bytes 368640 | tf_op jit(solution)/shard_map/all_gather | solution.py:437
  697.4 14.3 %all-gather.6 = f32[4,11,1024]{2,1,0:T(8,128)S(1)} all-gather(f32[1,11,1024]{2,1,0:T(8,128)S(1)} %bitcast.133), channel_id=4, replica_groups=mesh['seq'=8,'head'=4] {'head'}, dimensions={0}, use_global_device_ids=true | all-gather | bytes 225280 | tf_op jit(solution)/shard_map/all_gather | solution.py:437
  711.8 8.7 %all-gather.3 = f32[106496]{0:T(1024)S(1)} all-gather(f32[13312]{0:T(1024)S(1)} %pad_maximum_fusion.5), channel_id=5, replica_groups=mesh['seq'=8,'head'=4] {'seq'}, dimensions={0}, use_global_device_ids=true | all-gather | bytes 479232 | tf_op jit(solution)/shard_map/all_gather | solution.py:437
  (421 shorter events, 134.9 us)
Async XLA Ops:
  7.3 53.4 %all-gather.14.cloned.1.call-start = ((), (), s32[]{:S(2)}) async-start(), calls=%async_computation.7 | async-start | bytes 2621440 | tf_op jit(solution)/shard_map/all_gather | solution.py:417
  12.1 78.7 %all-gather.16.cloned.1.call-start = ((), (), s32[]{:S(2)}) async-start(), calls=%async_computation.8 | async-start | bytes 2654208 | tf_op jit(solution)/shard_map/all_gather | solution.py:508
  16.4 159.6 %all-gather.18.cloned.1.call-start = ((), (), s32[]{:S(2)}) async-start(), calls=%async_computation.9 | async-start | bytes 5308416 | tf_op jit(solution)/shard_map/all_gather | solution.py:524
  18.5 207.0 %reduce-scatter.8.cloned.1.call-start = ((), (), s32[]{:S(2)}) async-start(), calls=%async_computation.10 | async-start | bytes 2621440 | tf_op jit(solution)/shard_map/reduce_scatter | solution.py:421
  18.7 74.6 %copy-start.68 = (f32[1,1024]{1,0:T(1,128)}, f32[1,1024]{1,0:T(1,128)S(1)}, u32[]{:S(2)}) copy-start(f32[1,1024]{1,0:T(1,128)S(1)} %get-tuple-element.266) | copy-start | bytes 12292
  18.7 573.1 %copy-start.73 = (f32[1,1024]{1,0:T(1,128)}, f32[1,1024]{1,0:T(1,128)S(1)}, u32[]{:S(2)}) copy-start(f32[1,1024]{1,0:T(1,128)S(1)} %get-tuple-element.261) | copy-start | bytes 12292
  18.7 573.0 %copy-start.75 = (f32[1,1024]{1,0:T(1,128)}, f32[1,1024]{1,0:T(1,128)S(1)}, u32[]{:S(2)}) copy-start(f32[1,1024]{1,0:T(1,128)S(1)} %get-tuple-element.263) | copy-start | bytes 12292
  61.4 11.3 %collective-permute-start = (bf16[1,1024]{1,0:T(2,128)(2,1)S(1)}, bf16[1,1024]{1,0:T(2,128)(2,1)S(1)}, u32[]{:S(2)}, u32[]{:S(2)}) collective-permute-start(bf16[1,1024]{1,0:T(2,128)(2,1)S(1)} %slice.328), channel_id=1, source_target_pairs={{0,4},{4,8},{8,12},{12,16},{16,20},{20,24},{24,28},{1,5},{5,9},{9,... | collective-permute-start | bytes 6152 | tf_op jit(solution)/shard_map/ppermute | solution.py:342
  176.0 54.3 %copy-start.49 = (bf16[1024,256]{1,0:T(8,128)(2,1)}, bf16[1024,256]{1,0:T(8,128)(2,1)S(1)}, u32[]{:S(2)}) copy-start(bf16[1024,256]{1,0:T(8,128)(2,1)S(1)} %get-tuple-element.226) | copy-start | bytes 1572868
  176.0 52.1 %copy-start.72 = (f32[1024]{0:T(1024)S(1)}, f32[1024]{0:T(1024)}, u32[]{:S(2)}) copy-start(f32[1024]{0:T(1024)} %param.57) | copy-start | bytes 12292
  176.0 52.1 %copy-start.96 = (f32[1024]{0:T(1024)S(1)}, f32[1024]{0:T(1024)}, u32[]{:S(2)}) copy-start(f32[1024]{0:T(1024)} %param.58) | copy-start | bytes 12292
  179.3 99.1 %copy-start.107 = (f32[1024]{0:T(1024)S(1)}, f32[1024]{0:T(1024)}, u32[]{:S(2)}) copy-start(f32[1024]{0:T(1024)} %param.59) | copy-start | bytes 12292
  179.4 96.0 %all-gather.20.cloned.1.call-start = ((), (), s32[]{:S(2)}) async-start(), calls=%async_computation.11 | async-start | bytes 2621440 | tf_op jit(solution)/shard_map/all_gather | solution.py:417
  230.3 90.9 %all-gather.22.cloned.1.call-start = ((), (), s32[]{:S(2)}) async-start(), calls=%async_computation.13 | async-start | bytes 2621440 | tf_op jit(solution)/shard_map/all_gather | solution.py:417
  230.9 151.6 %reduce-scatter.12.cloned.1.call-start = ((), (), s32[]{:S(2)}) async-start(), calls=%async_computation.14 | async-start | bytes 2621440 | tf_op jit(solution)/shard_map/reduce_scatter | solution.py:421
  276.1 2.4 collective-permute-start.1
  333.0 3.0 collective-permute-start.2
  338.6 89.1 %reduce-scatter.10.cloned.1.call-start = ((), (), s32[]{:S(2)}) async-start(), calls=%async_computation.12 | async-start | bytes 2621440 | tf_op jit(solution)/shard_map/reduce_scatter | solution.py:421
  345.2 133.0 %all-gather.24.cloned.1.call-start = ((), (), s32[]{:S(2)}) async-start(), calls=%async_computation.15 | async-start | bytes 2621440 | tf_op jit(solution)/shard_map/all_gather | solution.py:417
  430.2 52.5 %copy-start.93 = (f32[256]{0:T(256)}, f32[256]{0:T(256)S(1)}, u32[]{:S(2)}) copy-start(f32[256]{0:T(256)S(1)} %negate_multiply_fusion.1) | copy-start | bytes 3076
  433.2 260.8 %reduce-scatter.14.cloned.1.call-start = ((), (), s32[]{:S(2)}) async-start(), calls=%async_computation.16 | async-start | bytes 2621440 | tf_op jit(solution)/shard_map/reduce_scatter | solution.py:421
  585.4 6.4 collective-permute-start.3
  625.7 14.8 %all-to-all-start.1 = ((bf16[8,36,256]{2,1,0:T(8,128)(2,1)}), bf16[8,36,256]{2,1,0:T(8,128)(2,1)}, u32[]{:S(2)}, u32[]{:S(2)}) async-start(bf16[8,36,256]{2,1,0:T(8,128)(2,1)} %pad_maximum_fusion.4), calls=%async_computation.5 | async-start | bytes 327680 | tf_op jit(solution)/shard_map/all_to_all | solution.py:736
  629.7 94.3 %reduce-scatter.16.cloned.1.call-start = ((), (), s32[]{:S(2)}) async-start(), calls=%async_computation.17 | async-start | bytes 5308416
  640.5 33.7 %all-to-all-start = ((bf16[8,128,1056]{1,2,0:T(8,128)(2,1)}), bf16[8,128,1056]{1,2,0:T(8,128)(2,1)}, u32[]{:S(2)}, u32[]{:S(2)}) async-start(bf16[8,128,1056]{1,2,0:T(8,128)(2,1)} %copy_bitcast_fusion), calls=%async_computation.4 | async-start | bytes 4325376 | tf_op jit(solution)/shard_map/all_to_all | solution.py:443
  644.9 50.6 %copy-start.92 = (f32[256]{0:T(256)S(1)}, f32[256]{0:T(256)}, u32[]{:S(2)}) copy-start(f32[256]{0:T(256)} %copy-done.91) | copy-start | bytes 3076
  644.9 50.6 %copy-start.89 = (f32[256]{0:T(256)S(1)}, f32[256]{0:T(256)}, u32[]{:S(2)}) copy-start(f32[256]{0:T(256)} %copy-done.88) | copy-start | bytes 3076
  647.2 50.0 %copy-start.84 = (f32[1024]{0:T(1024)S(1)}, f32[1024]{0:T(1024)}, u32[]{:S(2)}) copy-start(f32[1024]{0:T(1024)} %get-tuple-element.198) | copy-start | bytes 12292
  647.2 50.0 %copy-start.85 = (f32[1024]{0:T(1024)S(1)}, f32[1024]{0:T(1024)}, u32[]{:S(2)}) copy-start(f32[1024]{0:T(1024)} %get-tuple-element.199) | copy-start | bytes 12292
  647.3 50.0 %copy-start.86 = (f32[1024]{0:T(1024)S(1)}, f32[1024]{0:T(1024)}, u32[]{:S(2)}) copy-start(f32[1024]{0:T(1024)} %get-tuple-element.200) | copy-start | bytes 12292
  647.3 50.0 %copy-start.87 = (f32[1024]{0:T(1024)S(1)}, f32[1024]{0:T(1024)}, u32[]{:S(2)}) copy-start(f32[1024]{0:T(1024)} %get-tuple-element.201) | copy-start | bytes 12292
  647.3 50.0 %copy-start.99 = (f32[1024]{0:T(1024)S(1)}, f32[1024]{0:T(1024)}, u32[]{:S(2)}) copy-start(f32[1024]{0:T(1024)} %get-tuple-element.231) | copy-start | bytes 12292
  (111 other events, 1131.3 us)
Sparse Core Ops, SparseCore 0:
  12.2 48.3 all-gather.13
  63.1 27.6 all-gather.15
  92.7 39.6 all-gather.17
  179.5 46.0 reduce-scatter.7
  230.4 44.8 all-gather.19
  276.8 44.4 all-gather.21
  338.7 43.8 reduce-scatter.11
  384.8 42.8 reduce-scatter.9
  433.3 44.8 all-gather.23
  600.1 42.2 reduce-scatter.13
  645.9 52.9 reduce-scatter.15
